TPU v7x, 256 devices: a whole 4x4x8 slice. The times are simulated.
256 devices in a mesh: seq: 32 (over y, z_lo, core), kvh: 8 (over x, z_hi).
Axes of the slice: x: 4, y: 4, z: 8 (z_hi: 2, z_lo: 4; z = z_hi * 4 + z_lo), core: 2. Of those that a mesh axis runs over, the one named last changes fastest.
Arguments:
- queries: bfloat16 [8192, 8192], P('seq', 'kvh'), may hold values from -2.5 to 2.5
- key_vector_rows: bfloat16 [8192, 1024], P(('seq', 'kvh')), may hold values from -2.5 to 2.5
- value_vector_rows: bfloat16 [8192, 1024], P(('seq', 'kvh')), may hold values from -5 to 5
- output_gradient: bfloat16 [8192, 8192], P('seq', 'kvh'), may hold values from -24 to 24
- key_lists: int32 [64, 24], replicated, may hold values from 0 to 63, as said below
- block_counts: int32 [64], replicated, may hold values from 1 to 24, as said below
- span_table: int32 [64], replicated, may hold values from 0 to 63, each once
Outputs:
- grad_queries: bfloat16 [8192, 8192], P('seq', 'kvh')
- key_gradient: bfloat16 [8192, 1024], P(('seq', 'kvh'))
- value_gradient: bfloat16 [8192, 1024], P(('seq', 'kvh'))
Inputs may be any that keep to these rules, and one draw needn't show every extreme that they name: `key_lists`: row b lists, by position, the key blocks of query block b: its first block_counts[b] entries are distinct blocks at or before b, the first being b itself; the remaining entries are 0. block_counts[b] is at most b + 1 and at most 24; the last block's count is 24. `span_table`: each position block appears once.
All inputs are finite; a program needn't handle non-finite values.
Results may differ from a plain program's by a relative error of at most 0.0055.
Values may be sent and summed in bfloat16 or wider, within the bound.
A program may use at most 128 MiB of HBM per device.

v0:
```python
import jax
import jax.numpy as jnp
from jax import lax
from jax.sharding import PartitionSpec as P

HEAD_SIZE = 128
QUERY_PER_KEY = 8
BLOCK_TOKENS = 128


def shards(
    queries,
    key_vector_rows,
    value_vector_rows,
    output_gradient,
    key_lists,
    block_counts,
    span_table,
):
    key_heads, value_heads = (
        lax.all_to_all(key_vector_rows, "kvh", split_axis=1, concat_axis=0, tiled=True),
        lax.all_to_all(value_vector_rows, "kvh", split_axis=1, concat_axis=0, tiled=True),
    )
    keys_all, values_all = (
        lax.all_gather(key_heads, "seq", axis=0, tiled=True),
        lax.all_gather(value_heads, "seq", axis=0, tiled=True),
    )
    head_dim = HEAD_SIZE
    group_size = QUERY_PER_KEY
    block_rows = BLOCK_TOKENS
    logit_scale = HEAD_SIZE ** (-0.5)
    local_rows = queries.shape[0]
    local_blocks = local_rows // block_rows
    total_blocks = keys_all.shape[0] // block_rows
    queries_grouped = queries.reshape(local_rows, group_size, head_dim)
    grads_grouped = output_gradient.reshape(local_rows, group_size, head_dim)
    inverse = (
        jnp.zeros((total_blocks,), jnp.int32)
        .at[span_table]
        .set(jnp.arange(total_blocks, dtype=jnp.int32))
    )
    first_slot = lax.axis_index("seq") * local_blocks
    lower_mask = jnp.arange(block_rows)[None, :] <= jnp.arange(block_rows)[:, None]

    def block_scores(query_blk, key_pos, query_pos):
        row_start = inverse[key_pos] * block_rows
        key_blk = lax.dynamic_slice_in_dim(keys_all, row_start, block_rows, 0)
        value_blk = lax.dynamic_slice_in_dim(values_all, row_start, block_rows, 0)
        scores = (
            jnp.einsum("tgd,sd->gts", query_blk, key_blk, preferred_element_type=jnp.float32)
            * logit_scale
        )
        allowed = jnp.logical_or(key_pos != query_pos, lower_mask)
        return (scores, allowed, key_blk, value_blk, row_start)

    def forward_maker(query_blk, query_pos):

        def forward_step(entry_id, carried):
            row_total, weighted = carried
            key_pos = key_lists[query_pos, entry_id]
            scores, allowed, key_blk, value_blk, row_start = block_scores(
                query_blk, key_pos, query_pos
            )
            exp_scores = jnp.where(allowed, jnp.exp(scores), 0.0)
            row_total = row_total + jnp.sum(exp_scores, -1)
            weighted = weighted + jnp.einsum(
                "gts,sd->tgd",
                exp_scores.astype(jnp.bfloat16),
                value_blk,
                preferred_element_type=jnp.float32,
            )
            return (row_total, weighted)

        return forward_step

    prepared = []
    for index_local in range(local_blocks):
        query_blk = queries_grouped[index_local * block_rows : (index_local + 1) * block_rows]
        grad_blk = grads_grouped[index_local * block_rows : (index_local + 1) * block_rows]
        query_pos = span_table[first_slot + index_local]
        entries = block_counts[query_pos]
        starting_carry = (
            jnp.zeros((group_size, block_rows), jnp.float32),
            jnp.zeros((block_rows, group_size, head_dim), jnp.float32),
        )
        row_total, weighted = lax.fori_loop(
            0, entries, forward_maker(query_blk, query_pos), starting_carry
        )
        attended = weighted / jnp.transpose(row_total)[:, :, None]
        row_delta = jnp.transpose(jnp.sum(grad_blk.astype(jnp.float32) * attended, -1))
        prepared.append((query_blk, grad_blk, query_pos, entries, jnp.log(row_total), row_delta))

    def pair_grads(prepared_item, key_pos):
        query_blk, grad_blk, query_pos, entries, log_total, row_delta = prepared_item
        scores, allowed, key_blk, value_blk, row_start = block_scores(query_blk, key_pos, query_pos)
        weights = jnp.where(allowed, jnp.exp(scores - log_total[:, :, None]), 0.0)
        value_part = jnp.einsum(
            "gts,tgd->sd",
            weights.astype(jnp.bfloat16),
            grad_blk,
            preferred_element_type=jnp.float32,
        )
        weight_grads = jnp.einsum(
            "tgd,sd->gts", grad_blk, value_blk, preferred_element_type=jnp.float32
        )
        score_grads = (weights * (weight_grads - row_delta[:, :, None])).astype(jnp.bfloat16)
        query_part = jnp.einsum(
            "gts,sd->tgd", score_grads, key_blk, preferred_element_type=jnp.float32
        )
        key_part = jnp.einsum(
            "gts,tgd->sd", score_grads, query_blk, preferred_element_type=jnp.float32
        )
        return (query_part, jnp.concatenate([key_part, value_part], 1), row_start)

    def grad_maker(prepared_item):

        def grad_step(entry_id, carried):
            query_grad, buffer = carried
            query_part, pair_kv, row_start = pair_grads(
                prepared_item, key_lists[prepared_item[2], entry_id]
            )
            previous = lax.dynamic_slice_in_dim(buffer, row_start, block_rows, 0)
            buffer = lax.dynamic_update_slice_in_dim(buffer, previous + pair_kv, row_start, 0)
            return (query_grad + query_part, buffer)

        return grad_step

    zero_grad = jnp.zeros((block_rows, group_size, head_dim), jnp.float32)
    query_grads = []
    buffer = jnp.zeros((total_blocks * block_rows, 2 * head_dim), jnp.float32)
    for prepared_item in prepared:
        query_grad, buffer = lax.fori_loop(
            0, prepared_item[3], grad_maker(prepared_item), (zero_grad, buffer)
        )
        query_grads.append(query_grad)
    kv_sums = lax.psum_scatter(buffer, "seq", scatter_dimension=0, tiled=True)
    query_all = jnp.concatenate(query_grads, 0) * logit_scale
    grad_queries = query_all.reshape(local_rows, group_size * head_dim).astype(jnp.bfloat16)
    key_out = (kv_sums[:, :head_dim] * logit_scale).astype(jnp.bfloat16)
    value_out = kv_sums[:, head_dim:].astype(jnp.bfloat16)
    key_gradient, value_gradient = (
        lax.all_to_all(key_out, "kvh", split_axis=0, concat_axis=1, tiled=True),
        lax.all_to_all(value_out, "kvh", split_axis=0, concat_axis=1, tiled=True),
    )
    return (grad_queries, key_gradient, value_gradient)


def solution(mesh):
    placed = (
        P("seq", "kvh"),
        P(("seq", "kvh"), None),
        P(("seq", "kvh"), None),
        P("seq", "kvh"),
        P(),
        P(),
        P(),
    )
    return jax.shard_map(
        shards,
        mesh=mesh,
        in_specs=placed,
        out_specs=(P("seq", "kvh"), P(("seq", "kvh"), None), P(("seq", "kvh"), None)),
        check_vma=False,
    )
```

profile of v0, /device:TPU:2, one launch (start us, length us, event | category | flops | bytes accessed | tf_op | source)
XLA Modules:
  0.0 1217.7 jit_solution(8406833284898514039)
XLA Ops:
  8.0 20.2 %all_to_all.76 = bf16[32,8,128]{2,0,1:T(8,128)(2,1)} all-to-all(bf16[32,8,128]{2,0,1:T(8,128)(2,1)S(1)} %copy_bitcast_fusion.2), channel_id=1, replica_groups=mesh['seq'=32,'kvh'=8] {'kvh'}, dimensions={1} | all-to-all | bytes 131072 | tf_op jit(solution)/shard_map/all_to_all | solution.py:22
  29.1 13.3 %all_to_all.77 = bf16[32,8,128]{2,0,1:T(8,128)(2,1)} all-to-all(bf16[32,8,128]{2,0,1:T(8,128)(2,1)S(1)} %copy_bitcast_fusion.3), channel_id=1, replica_groups=mesh['seq'=32,'kvh'=8] {'kvh'}, dimensions={1} | all-to-all | bytes 131072 | tf_op jit(solution)/shard_map/all_to_all | solution.py:21
  51.4 34.0 %all-gather.5.cloned.1.call-done = bf16[8192,128]{1,0:T(8,128)(2,1)} async-done(((bf16[256,128]{1,0:T(8,128)(2,1)}), bf16[8192,128]{1,0:T(8,128)(2,1)}) %all-gather.5.cloned.1.call-update) | async-done | bytes 2097168 | tf_op jit(solution)/shard_map/all_gather | solution.py:26
  85.4 4.1 copy.112
  89.5 56.8 %all-gather.3.cloned.1.call-done = bf16[8192,128]{1,0:T(8,128)(2,1)} async-done(((bf16[256,128]{1,0:T(8,128)(2,1)}), bf16[8192,128]{1,0:T(8,128)(2,1)}) %all-gather.3.cloned.1.call-update) | async-done | bytes 2097168 | tf_op jit(solution)/shard_map/all_gather | solution.py:25
  146.3 177.8 %while.62 = (s32[]{:T(128)}, f32[8,128]{1,0:T(8,128)S(1)}, f32[128,8,128]{0,2,1:T(8,128)S(1)}, s32[]{:T(128)}, s32[64,24]{0,1:T(8,128)}, /*index=5*/s32[]{:T(128...) while((s32[]{:T(128)}, f32[8,128]{1,0:T(8,128)S(1)}, ...), condition=%wide.region_9.10_spmd.clone, body=%wide.region_7.0_spmd.clone.sunk | while | flops 67797008 | bytes 1950017 | solution.py:86
  324.2 118.4 %while.60 = (s32[]{:T(128)}, f32[8,128]{1,0:T(8,128)S(1)}, f32[128,8,128]{0,2,1:T(8,128)S(1)}, s32[]{:T(128)}, s32[64,24]{0,1:T(8,128)}, /*index=5*/s32[]{:T(128...) while((s32[]{:T(128)}, f32[8,128]{1,0:T(8,128)S(1)}, ...), condition=%wide.region_3.4_spmd.clone, body=%wide.region_1.3_spmd.clone.sunk | while | flops 67797008 | bytes 1950017 | solution.py:86
  442.8 4.2 broadcast_in_dim.56
  447.0 160.8 %while.61 = (s32[]{:T(128)}, f32[128,8,128]{0,2,1:T(8,128)S(1)}, f32[8192,256]{0,1:T(8,128)}, s32[]{:T(128)}, s32[64,24]{0,1:T(8,128)}, /*index=5*/s32[]{:T(128)...) while((s32[]{:T(128)}, f32[128,8,128]{0,2,1:T(8,128)S(1)}, ...), condition=%wide.region_6.0_spmd.clone, body=%wide.region_5.6_spmd.clone.sunk | while | flops 168919056 | bytes 5120353 | solution.py:132
  514.0 1.6 fusion.164
  525.5 1.6 fusion.164
  548.4 1.6 fusion.164
  608.0 243.2 %while.63 = (s32[]{:T(128)}, f32[128,8,128]{0,2,1:T(8,128)S(1)}, f32[8192,256]{0,1:T(8,128)}, s32[]{:T(128)}, s32[64,24]{0,1:T(8,128)}, /*index=5*/s32[]{:T(128)...) while((s32[]{:T(128)}, f32[128,8,128]{0,2,1:T(8,128)S(1)}, ...), condition=%wide.region_12.13_spmd.clone, body=%wide.region_11.12_spmd.clone.sunk | while | flops 168919056 | bytes 5120353 | solution.py:132
  675.6 1.6 fusion.185
  744.9 1.6 fusion.185
  768.0 1.6 fusion.185
  791.1 1.6 fusion.185
  802.7 1.6 fusion.185
  851.2 9.0 copy.120
  861.5 318.3 %reduce-scatter.2.cloned.1.call-done = f32[256,256]{1,0:T(8,128)} async-done(((f32[8192,256]{1,0:T(8,128)}), f32[256,256]{1,0:T(8,128)}) %reduce-scatter.2.cloned.1.call-update) | async-done | bytes 262160 | tf_op jit(solution)/shard_map/reduce_scatter | solution.py:136
  1181.3 6.9 all-to-all-start.3
  1189.8 7.3 all-to-all-done.3
  1197.0 4.7 all-to-all-start.2
  1202.4 8.2 all-to-all-done.2
  (563 shorter events, 382.1 us)
Async XLA Ops:
  7.2 0.8 copy-start
  7.2 41.1 %copy-start.1 = (bf16[256,1024]{1,0:T(8,128)(2,1)S(1)}, bf16[256,1024]{1,0:T(8,128)(2,1)}, u32[]{:S(2)}) copy-start(bf16[256,1024]{1,0:T(8,128)(2,1)} %param.18) | copy-start | bytes 1572868
  7.2 78.2 %all-gather.5.cloned.1.call-start = ((), (), s32[]{:S(2)}) async-start(), calls=%async_computation.6 | async-start | bytes 2162688 | tf_op jit(solution)/shard_map/all_gather | solution.py:26
  28.2 118.1 %all-gather.3.cloned.1.call-start = ((), (), s32[]{:S(2)}) async-start(), calls=%async_computation.5 | async-start | bytes 2162688 | tf_op jit(solution)/shard_map/all_gather | solution.py:25
  42.5 1137.3 %reduce-scatter.2.cloned.1.call-start = ((), (), s32[]{:S(2)}) async-start(), calls=%async_computation.7 | async-start | bytes 8650752 | tf_op jit(solution)/shard_map/reduce_scatter | solution.py:136
  47.5 2.5 copy-start.2
  47.5 3.3 copy-start.3
  1181.3 15.7 %all-to-all-start.3 = ((bf16[8,32,128]{2,1,0:T(8,128)(2,1)}), bf16[8,32,128]{2,1,0:T(8,128)(2,1)S(1)}, u32[]{:S(2)}, u32[]{:S(2)}) async-start(bf16[8,32,128]{2,1,0:T(8,128)(2,1)} %bitcast.20), calls=%async_computation.4 | async-start | bytes 131072 | tf_op jit(solution)/shard_map/all_to_all | solution.py:143
  1197.0 13.6 %all-to-all-start.2 = ((bf16[8,32,128]{2,1,0:T(8,128)(2,1)}), bf16[8,32,128]{2,1,0:T(8,128)(2,1)S(1)}, u32[]{:S(2)}, u32[]{:S(2)}) async-start(bf16[8,32,128]{2,1,0:T(8,128)(2,1)} %bitcast.18), calls=%async_computation.3 | async-start | bytes 131072 | tf_op jit(solution)/shard_map/all_to_all | solution.py:142
Sparse Core Ops, SparseCore 0:
  28.3 57.0 all-gather.4
  87.3 58.9 all-gather.2
  860.3 319.4 reduce-scatter.1
where the time goes:
time: 1240 us; the launch traced here: 1220 us
  waiting for transfers between devices  425 us (34%)
  loops' own time  318 us (26%)
  matrix products  193 us (16%)
  local copies, waits for them, and re-layouts  159 us (13%)
  other arithmetic  60 us (5%)
  blocking collectives  33.5 us (3%)
  between operations  17.8 us (1%)
    reduce_scatter x1, waiting for transfers between devices, shards(): kv_sums = lax.psum_scatter(buffer, 'seq', scatter_dimension=0, tiled=True)  318 us
    another operation x2, loops' own time, shards(): lax.fori_loop(0, prepared_item[3], grad_maker(prepared_item), (zero_grad,...  160 us
    another operation x2, loops' own time, shards(): lax.fori_loop(0, entries, forward_maker(query_blk, query_pos), starting_c...  158 us
    dot_general x70, matrix products, block_scores(): jnp.einsum('tgd,sd->gts', query_blk, key_blk, preferred_element_type=jnp....  72 us
    all_gather x1, waiting for transfers between devices, shards(): lax.all_gather(key_heads, 'seq', axis=0, tiled=True)  56.8 us
    dynamic_update_slice x35, other arithmetic, grad_step(): lax.dynamic_update_slice_in_dim(buffer, previous + pair_kv, row_start, 0)  56 us
    dynamic_slice x35, local copies, waits for them, and re-layouts, forward_step(): key_pos = key_lists[query_pos, entry_id]  45.1 us
    dynamic_slice x35, local copies, waits for them, and re-layouts, grad_step(): key_lists[prepared_item[2], entry_id]  44.9 us
  transfers between devices with their start and end apart: 5, of which 5 were waited for; matrix products, arithmetic and copies ran while one was open for 1% of the time, Pallas kernels for 0%

commit v1 on v0

v1 whole, which is shorter than its diff:
```python
import jax
import jax.numpy as jnp
from jax import lax
from jax.experimental import pallas as pl
from jax.experimental.pallas import tpu as pltpu
from jax.sharding import PartitionSpec as P
H = 128
G = 8
B = 128
NB = 24
NBLK = 64
SC = H ** -0.5
C2 = SC * 1.4426950408889634
R = G * B
bf = jnp.bfloat16
f32 = jnp.float32


def attn_kernel(slots, counts, inv, q_ref, do_ref, kv_ref, dq_ref, part,
                qT, doT, qr, dor, e_buf, p_buf, dkb, dvb, dqT):
    dkb[2 * NB] = jnp.zeros((B, H), f32)
    dvb[2 * NB] = jnp.zeros((B, H), f32)
    for j in range(2):
        for g in range(G):
            qb = q_ref[j * B:(j + 1) * B, g * H:(g + 1) * H]
            ob = do_ref[j * B:(j + 1) * B, g * H:(g + 1) * H]
            qr[g * B:(g + 1) * B, :] = qb
            dor[g * B:(g + 1) * B, :] = ob
            qT[:, g * B:(g + 1) * B] = qb.T
            doT[:, g * B:(g + 1) * B] = ob.T
        n = counts[j]

        def block(kv, e):
            s = slots[j * NB + e]
            return kv_ref[s // 2, kv, pl.ds(pl.multiple_of((s % 2) * B, B), B), :]

        def first(e, acc, diag):
            r, d = acc
            s = jnp.dot(block(0, e), qT[...], preferred_element_type=f32)
            x = jnp.exp2(s * C2)
            if diag:
                key = lax.broadcasted_iota(jnp.int32, (B, R), 0)
                qry = lax.broadcasted_iota(jnp.int32, (B, R), 1) % B
                x = jnp.where(key <= qry, x, 0.0)
            e_buf[e] = x
            p = jnp.dot(block(1, e), doT[...], preferred_element_type=f32)
            p_buf[e] = p
            r = r + jnp.sum(x.reshape(B // 8, 8, R), 0)
            d = d + jnp.sum((x * p).reshape(B // 8, 8, R), 0)
            return r, d

        z = jnp.zeros((8, R), f32)
        acc = first(0, (z, z), True)
        r, d = lax.fori_loop(1, n, lambda e, a: first(e, a, False), acc)
        rinv = 1.0 / jnp.sum(r, 0, keepdims=True)
        delta = jnp.sum(d, 0, keepdims=True) * rinv
        dqT[...] = jnp.zeros_like(dqT)

        def second(e, _):
            w = e_buf[e] * rinv
            dvb[j * NB + e] = jnp.dot(w.astype(bf), dor[...], preferred_element_type=f32)
            ds = (w * (p_buf[e] - delta)).astype(bf)
            dkb[j * NB + e] = jnp.dot(ds, qr[...], preferred_element_type=f32) * SC
            dqT[...] += lax.dot_general(block(0, e), ds, (((0,), (0,)), ((), ())), preferred_element_type=f32)
            return 0

        lax.fori_loop(0, n, second, 0)
        for g in range(G):
            dq_ref[j * B:(j + 1) * B, g * H:(g + 1) * H] = (dqT[:, g * B:(g + 1) * B].T * SC).astype(bf)

    def out(s, _):
        a, b = inv[s], inv[NBLK + s]
        i = s // 2
        c, y, z = i % 2, i // 8, (i // 2) % 4
        rows = pl.ds(pl.multiple_of((s % 2) * B, B), B)
        part[c, y, z, 0, rows, :] = (dkb[a] + dkb[b]).astype(bf)
        part[c, y, z, 1, rows, :] = (dvb[a] + dvb[b]).astype(bf)
        return 0

    lax.fori_loop(0, NBLK, out, 0)


def attn(slots, counts, inv, q, do, kv):
    vm = pl.BlockSpec(memory_space=pltpu.VMEM)
    sm = pl.BlockSpec(memory_space=pltpu.SMEM)
    return pl.pallas_call(
        attn_kernel,
        out_shape=(jax.ShapeDtypeStruct((2 * B, R), bf), jax.ShapeDtypeStruct((2, 4, 4, 2, 2 * B, H), bf)),
        in_specs=[sm] * 3 + [vm] * 3,
        out_specs=[vm] * 2,
        scratch_shapes=[pltpu.VMEM((H, R), bf)] * 2 + [pltpu.VMEM((R, H), bf)] * 2
        + [pltpu.VMEM((NB, B, R), f32)] * 2 + [pltpu.VMEM((2 * NB + 1, B, H), f32)] * 2 + [pltpu.VMEM((H, R), f32)],
        compiler_params=pltpu.CompilerParams(vmem_limit_bytes=58 << 20),
    )(slots, counts, inv, q, do, kv)


def tables(key_lists, block_counts, span_table, first):
    qpos = lax.dynamic_slice_in_dim(span_table, first, 2)
    lists = key_lists[qpos]
    counts = block_counts[qpos]
    slots = jnp.argmax(span_table[None, None, :] == lists[:, :, None], -1).astype(jnp.int32)
    ent = jnp.arange(NB, dtype=jnp.int32)
    hit = (span_table[None, :, None] == lists[:, None, :]) & (ent[None, None, :] < counts[:, None, None])
    base = jnp.arange(2, dtype=jnp.int32)[:, None] * NB
    idx = jnp.where(hit.any(-1), jnp.argmax(hit, -1).astype(jnp.int32) + base, 2 * NB)
    return slots.reshape(-1), counts, idx.reshape(-1)

MESH = pl.DeviceIdType.MESH
bf = jnp.bfloat16; f32 = jnp.float32
NK = 8

def place():
    i = lax.axis_index("seq"); j = lax.axis_index("kvh")
    return i, j, i // 8, (i // 2) % 4, i % 2

def seq_of(y, z, c):
    return (y * 4 + z) * 2 + c

def zrel(z):
    return [z, z + 1 - 2 * (z % 2), (z + 2) % 4, 3 - z]

def enter(i, j, y, z, c):
    zs = zrel(z)
    barrier = pltpu.get_barrier_semaphore()
    seqs = [seq_of(y, z, 1 - c)] + [seq_of(y, zs[r], c) for r in (1, 2, 3)] + [seq_of((y + 1) % 4, z, c), seq_of((y + 3) % 4, z, c)]
    for s in seqs:
        pl.semaphore_signal(barrier, inc=1, device_id=(s, j), device_id_type=MESH)
    for d in range(1, NK):
        pl.semaphore_signal(barrier, inc=1, device_id=(i, (j + d) % NK), device_id_type=MESH)
    pl.semaphore_wait(barrier, len(seqs) + NK - 1)

def rcopy(src, dst, ss, rs, dev):
    return pltpu.make_async_remote_copy(src_ref=src, dst_ref=dst, send_sem=ss, recv_sem=rs, device_id=dev, device_id_type=MESH)

def gather_kernel(k_ref, v_ref, all_ref, tx, hs, hr, zs_, zr_, ys, yr, hfs, hfr, cs, cr):
    i, j, y, z, c = place()
    enter(i, j, y, z, c)
    zz = zrel(z)
    for h in range(NK):
        tx[h, 0] = k_ref[:, h*128:(h+1)*128]
        tx[h, 1] = v_ref[:, h*128:(h+1)*128]
    rows = pl.ds(pl.multiple_of(j * 32, 32), 32)
    ops = []
    for d in range(1, NK):
        h = (j + d) % NK
        cp = rcopy(tx.at[h], all_ref.at[i, :, rows, :], hs.at[d-1], hr.at[d-1], (i, h)); cp.start(); ops.append(cp)
    all_ref[i, 0, rows, :] = tx[j, 0]
    all_ref[i, 1, rows, :] = tx[j, 1]
    for cp in ops: cp.wait_recv()
    sends = list(ops)
    sib = (seq_of(y, z, 1 - c), j)
    up = (seq_of((y + 1) % 4, z, c), j)
    dn = (seq_of((y + 3) % 4, z, c), j)
    def send(src, dst, ss, rs, dev):
        cp = rcopy(src, dst, ss, rs, dev); cp.start(); sends.append(cp); return cp
    def chunk(yy, r):
        return all_ref.at[seq_of(yy % 4, zz[r], c)]
    n_c = [0]
    sibs = []
    def to_sib(yy, r):
        n = n_c[0]; n_c[0] += 1
        sibs.append(send(chunk(yy, r), chunk(yy, r), cs.at[n], cr.at[n], sib))
    zc, uc, dc, huc, hdc = [None]*4, [], [], [], []
    for r in range(4):
        if r == 0:
            for q in (1, 2, 3):
                zc[q] = send(chunk(y, 0), chunk(y, 0), zs_.at[q-1], zr_.at[q-1], (seq_of(y, zz[q], c), j))
        else:
            zc[r].wait_recv()
        uc.append(send(chunk(y, r), chunk(y, r), ys.at[0, r], yr.at[0, r], up))
        dc.append(send(chunk(y, r), chunk(y, r), ys.at[1, r], yr.at[1, r], dn))
        to_sib(y, r)
    for r in range(4):
        uc[r].wait_recv()
        s = seq_of((y + 3) % 4, zz[r], c)
        huc.append(send(all_ref.at[s, 0], all_ref.at[s, 0], hfs.at[0, r], hfr.at[0, r], up))
        to_sib(y + 3, r)
        dc[r].wait_recv()
        s = seq_of((y + 1) % 4, zz[r], c)
        hdc.append(send(all_ref.at[s, 1], all_ref.at[s, 1], hfs.at[1, r], hfr.at[1, r], dn))
        to_sib(y + 1, r)
    for r in range(4):
        huc[r].wait_recv()
        hdc[r].wait_recv()
        to_sib(y + 2, r)
    for cp in sibs: cp.wait_recv()
    for cp in sends: cp.wait_send()

def gather(k, v, cid=0):
    vm = pl.BlockSpec(memory_space=pltpu.VMEM)
    D = pltpu.SemaphoreType.DMA
    return pl.pallas_call(gather_kernel, out_shape=jax.ShapeDtypeStruct((32, 2, 256, 128), bf),
        in_specs=[vm, vm], out_specs=vm,
        scratch_shapes=[pltpu.VMEM((NK, 2, 32, 128), bf), D((7,)), D((7,)), D((3,)), D((3,)), D((2, 4)), D((2, 4)), D((2, 4)), D((2, 4)), D((16,)), D((16,))],
        compiler_params=pltpu.CompilerParams(collective_id=cid, has_side_effects=True, vmem_limit_bytes=32 << 20))(k, v)

ORDER = (1, 2, 3, 0)

def reduce_kernel(part, ko_ref, vo_ref, rx0, acc, rxa, rxb, rxz, zsrc, res, rxh,
                  s0, r0, sa, ra, sb, rb, sz, rz, sh, rh):
    i, j, y, z, c = place()
    enter(i, j, y, z, c)
    zz = zrel(z)
    yy = [(y + 2) % 4, (y + 1) % 4, (y + 3) % 4, y]
    sib = (seq_of(y, z, 1 - c), j)
    up = (seq_of(yy[1], z, c), j)
    dn = (seq_of(yy[2], z, c), j)
    sends = []
    def send(src, dst, ss, rs, dev):
        cp = rcopy(src, dst, ss, rs, dev); cp.start(); sends.append(cp); return cp
    c0 = [send(part.at[1 - c, yy[g]], rx0.at[g], s0.at[g], r0.at[g], sib) for g in range(4)]
    def tiles(fn):
        def body(t, _):
            fn(pl.ds(pl.multiple_of(t * 64, 64), 64)); return 0
        lax.fori_loop(0, 4, body, 0)
    def base(g, r):
        def one(sl):
            for kv in range(2):
                acc[g, r, kv, sl, :] = (part[c, yy[g], zz[r], kv, sl, :].astype(f32) + rx0[g, zz[r], kv, sl, :].astype(f32)).astype(bf)
        tiles(one)
    c0[0].wait_recv()
    ca = [[None]*4, [None]*4]
    for r in ORDER:
        base(0, r)
        ca[0][r] = send(acc.at[0, r, 0], rxa.at[0, r], sa.at[0, r], ra.at[0, r], up)
        ca[1][r] = send(acc.at[0, r, 1], rxa.at[1, r], sa.at[1, r], ra.at[1, r], dn)
    cb = {}
    c0[1].wait_recv()
    c0[2].wait_recv()
    for r in ORDER:
        base(1, r)
        cb[0, r, 1] = send(acc.at[1, r, 1], rxb.at[0, r, 1], sb.at[0, r, 1], rb.at[0, r, 1], up)
        base(2, r)
        cb[1, r, 0] = send(acc.at[2, r, 0], rxb.at[1, r, 0], sb.at[1, r, 0], rb.at[1, r, 0], dn)
    for r in ORDER:
        ca[0][r].wait_recv()
        def addk(sl, r=r):
            acc[1, r, 0, sl, :] = (acc[1, r, 0, sl, :].astype(f32) + rxa[0, r, sl, :].astype(f32)).astype(bf)
        tiles(addk)
        cb[0, r, 0] = send(acc.at[1, r, 0], rxb.at[0, r, 0], sb.at[0, r, 0], rb.at[0, r, 0], up)
        ca[1][r].wait_recv()
        def addv(sl, r=r):
            acc[2, r, 1, sl, :] = (acc[2, r, 1, sl, :].astype(f32) + rxa[1, r, sl, :].astype(f32)).astype(bf)
        tiles(addv)
        cb[1, r, 1] = send(acc.at[2, r, 1], rxb.at[1, r, 1], sb.at[1, r, 1], rb.at[1, r, 1], dn)
    c0[3].wait_recv()
    cz = [None] * 4
    for r in ORDER:
        for side in range(2):
            for kv in range(2):
                cb[side, r, kv].wait_recv()
        def total(sl, r=r):
            for kv in range(2):
                t = part[c, y, zz[r], kv, sl, :].astype(f32) + rx0[3, zz[r], kv, sl, :].astype(f32) + rxb[0, r, kv, sl, :].astype(f32) + rxb[1, r, kv, sl, :].astype(f32)
                if r: acc[3, r, kv, sl, :] = t.astype(bf)
                else: zsrc[kv, sl, :] = t
        tiles(total)
        if r: cz[r] = send(acc.at[3, r], rxz.at[r-1], sz.at[r-1], rz.at[r-1], (seq_of(y, zz[r], c), j))
    for r in (1, 2, 3): cz[r].wait_recv()
    for h in range(NK):
        for kv in range(2):
            sl = slice(h*32, h*32+32)
            t = zsrc[kv, sl, :]
            for r in range(3): t = t + rxz[r, kv, sl, :].astype(f32)
            res[h, kv] = t.astype(bf)
    ch = []
    for d in range(1, NK):
        h = (j + d) % NK
        ch.append(send(res.at[h], rxh.at[NK - d], sh.at[d-1], rh.at[d-1], (i, h)))
    for d in range(NK):
        src = (j + d) % NK
        col = pl.ds(pl.multiple_of(src * 128, 128), 128)
        if d == 0:
            ko_ref[:, col] = res[j, 0]
            vo_ref[:, col] = res[j, 1]
        else:
            ch[NK - d - 1].wait_recv()
            ko_ref[:, col] = rxh[d, 0]
            vo_ref[:, col] = rxh[d, 1]
    for cp in sends: cp.wait_send()

def reduce(part, cid=1):
    vm = pl.BlockSpec(memory_space=pltpu.VMEM)
    D = pltpu.SemaphoreType.DMA
    V = pltpu.VMEM
    return pl.pallas_call(reduce_kernel, out_shape=(jax.ShapeDtypeStruct((32, 1024), bf),)*2,
        in_specs=[vm], out_specs=[vm, vm],
        scratch_shapes=[V((4, 4, 2, 256, 128), bf), V((4, 4, 2, 256, 128), bf), V((2, 4, 256, 128), bf), V((2, 4, 2, 256, 128), bf), V((3, 2, 256, 128), bf),
            V((2, 256, 128), f32), V((NK, 2, 32, 128), bf), V((NK, 2, 32, 128), bf),
            D((4,)), D((4,)), D((2, 4)), D((2, 4)), D((2, 4, 2)), D((2, 4, 2)), D((3,)), D((3,)), D((7,)), D((7,))],
        compiler_params=pltpu.CompilerParams(collective_id=cid, has_side_effects=True, vmem_limit_bytes=40 << 20))(part)


def shards(queries, key_vector_rows, value_vector_rows, output_gradient, key_lists, block_counts, span_table):
    slots, counts, inv = tables(key_lists, block_counts, span_table, lax.axis_index("seq") * 2)
    kv = gather(key_vector_rows, value_vector_rows)
    grad_queries, part = attn(slots, counts, inv, queries, output_gradient, kv)
    key_gradient, value_gradient = reduce(part)
    return (grad_queries, key_gradient, value_gradient)


def solution(mesh):
    tokens = P(("seq", "kvh"), None)
    heads = P("seq", "kvh")
    return jax.shard_map(
        shards,
        mesh=mesh,
        in_specs=(heads, tokens, tokens, heads, P(), P(), P()),
        out_specs=(heads, tokens, tokens),
        check_vma=False,
    )
```

time: 1240 us -> 130 us (0.10); the launches traced: 1220 us -> 129 us
  waiting for transfers between devices: 425 us -> 0 us
  loops' own time: 318 us -> 0 us
  matrix products: 193 us -> 0 us
  local copies, waits for them, and re-layouts: 159 us -> 10.2 us
  Pallas kernels: 0 us -> 114 us
  other arithmetic: 60 us -> 4.29 us
  blocking collectives: 33.5 us -> 0 us
  between operations: 17.8 us -> 0.7 us
    reduce_scatter x1 -> x0, waiting for transfers between devices: 318 us -> none  [shards(): kv_sums = lax.psum_scatter(buffer, 'seq', scatter_dimension=0, tiled=True)]
    another operation x4 -> x0, loops' own time: 318 us -> none  [the longest x2 160 us: shards(): lax.fori_loop(0, prepared_item[3], grad_maker(prepared_item), (zero_grad,...]
    dot_general x245 -> x0, matrix products: 193 us -> none  [the longest x70 72 us: block_scores(): jnp.einsum('tgd,sd->gts', query_blk, key_blk, preferred_element_type=jnp....]
    dynamic_slice x142 -> x0, local copies, waits for them, and re-layouts: 134 us -> none  [the longest x35 45.1 us: forward_step(): key_pos = key_lists[query_pos, entry_id]]
    pallas_call x0 -> x3, Pallas kernels: none -> 114 us  [the longest x1 44.9 us: reduce(): pl.pallas_call(reduce_kernel, out_shape=(jax.ShapeDtypeStruct((32, 1024),...]
    all_gather x2 -> x0, waiting for transfers between devices: 90.8 us -> none  [the longest x1 56.8 us: shards(): lax.all_gather(key_heads, 'seq', axis=0, tiled=True)]
    dynamic_update_slice x35 -> x0, other arithmetic: 56 us -> none  [grad_step(): lax.dynamic_update_slice_in_dim(buffer, previous + pair_kv, row_start, 0)]
    all_to_all x2 -> x0, blocking collectives: 33.5 us -> none  [the longest x1 20.2 us: shards(): lax.all_to_all(value_vector_rows, 'kvh', split_axis=1, concat_axis=0, til...]
  transfers between devices with their start and end apart: 5 -> 0, of which waited for: 5 -> 0; matrix products, arithmetic and copies ran while one was open for 1% -> 0% of each run, Pallas kernels for 0% -> 0%
where the time goes in v1:
time: 130 us; the launch traced here: 129 us
  Pallas kernels  114 us (88%)
  local copies, waits for them, and re-layouts  10.2 us (8%)
  other arithmetic  4.29 us (3%)
    pallas_call x1, Pallas kernels, reduce(): pl.pallas_call(reduce_kernel, out_shape=(jax.ShapeDtypeStruct((32, 1024),...  44.9 us
    pallas_call x1, Pallas kernels, gather(): pl.pallas_call(gather_kernel, out_shape=jax.ShapeDtypeStruct((32, 2, 256,...  37 us
    pallas_call x1, Pallas kernels, attn(): pl.pallas_call(attn_kernel, out_shape=(jax.ShapeDtypeStruct((2 * B, R), b...  31.7 us
    unnamed x15, local copies, waits for them, and re-layouts  7.85 us

profile of v1, /device:TPU:2, one launch (start us, length us, event | category | flops | bytes accessed | tf_op | source)
XLA Modules:
  0.0 128.8 jit_solution(5950800545273390864)
XLA Ops:
  0.6 0.0 copy-start
  0.6 0.7 compare_select_fusion
  1.4 0.0 copy-done
  1.4 0.6 gather_fusion.1
  2.0 0.1 iota_compare_fusion
  2.1 0.8 copy.12
  2.9 0.6 gather_fusion
  3.5 0.7 fusion
  4.2 1.3 iota_reduce_fusion
  5.5 0.1 add_select_fusion
  5.6 0.6 reshape.43.inv
  6.1 1.4 %iota_reduce_fusion.1 = (pred[2,24]{1,0:T(4,128)(4,1)}, s32[2,24]{1,0:T(2,128)S(1)}) fusion(s32[2,24]{1,0:T(2,128)S(1)} %gather_fusion, s32[64]{0:T(128)} %param.13), kind=kLoop, calls=%fused_computation.3 | loop fusion | flops 24240 | bytes 688 | tf_op jit(solution)/shard_map/tables/reduce | solution.py:101
  7.5 0.6 reshape.42.slots
  8.1 0.8 copy-done.3
  8.9 0.8 copy-done.4
  9.8 37.0 %shard_map.94.kv_ref = bf16[32,2,256,128]{3,2,1,0:T(8,128)(2,1)S(1)} custom-call(bf16[32,1024]{1,0:T(8,128)(2,1)S(1)} %copy-done.3, bf16[32,1024]{1,0:T(8,128)(2,1)S(1)} %copy-done.4), custom_call_target="tpu_custom_call" | custom-call | tf_op jit(solution)/shard_map/pallas_call | solution.py:192
  46.8 0.0 copy-done.5
  46.8 0.0 copy-start.1
  46.8 1.9 %copy-done.1 = bf16[32,2,256,128]{3,2,1,0:T(8,128)(2,1)} copy-done((bf16[32,2,256,128]{3,2,1,0:T(8,128)(2,1)}, bf16[32,2,256,128]{3,2,1,0:T(8,128)(2,1)S(1)}, u32[]{:S(2)}) %copy-start.1) | copy-done | bytes 4194328
  48.8 31.7 %shard_map.95 = (bf16[256,1024]{1,0:T(8,128)(2,1)}, bf16[2,4,4,2,256,128]{5,4,3,2,1,0:T(8,128)(2,1)}) custom-call(s32[48]{0:T(128)} %reshape.42.slots, s32[2]{0:T(128)} %copy-done.5, s32[128]{0:T(128)} %reshape.43.inv, bf16[256,1024]{1,0:T(8,128)(2,1)} %q_ref.1, bf16[256,1024]{1,0:T(8,128)(2,1)} %do_ref.1, bf16[32,2,256,128]{3,2,1,0:T(8,128)(2,1)} %copy-done.1), custom_call_target="tpu_custom_call" | custom-call | tf_op jit(solution)/shard_map/pallas_call | solution.py:86
  80.4 2.2 %copy-done.2 = bf16[2,4,4,2,256,128]{5,4,3,2,1,0:T(8,128)(2,1)S(1)} copy-done((bf16[2,4,4,2,256,128]{5,4,3,2,1,0:T(8,128)(2,1)S(1)}, bf16[2,4,4,2,256,128]{5,4,3,2,1,0:T(8,128)(2,1)}, u32[]{:S(2)}) %copy-start.2) | copy-done | bytes 4194328
  82.6 44.9 %shard_map.96 = (bf16[32,1024]{1,0:T(8,128)(2,1)S(1)}, bf16[32,1024]{1,0:T(8,128)(2,1)S(1)}) custom-call(bf16[2,4,4,2,256,128]{5,4,3,2,1,0:T(8,128)(2,1)S(1)} %copy-done.2), custom_call_target="tpu_custom_call" | custom-call | tf_op jit(solution)/shard_map/pallas_call | solution.py:286
  127.5 0.6 copy.15
  128.2 0.6 copy.16
  (6 shorter events, 0.0 us)
Async XLA Ops:
  0.6 0.8 copy-start
  2.0 44.8 %copy-start.5 = (s32[2]{0:T(128)}, s32[2]{0:T(128)S(1)}, u32[]{:S(2)}) copy-start(s32[2]{0:T(128)S(1)} %gather_fusion.1) | copy-start | bytes 28
  8.1 0.8 copy-start.3
  8.9 0.8 copy-start.4
  46.8 1.9 %copy-start.1 = (bf16[32,2,256,128]{3,2,1,0:T(8,128)(2,1)}, bf16[32,2,256,128]{3,2,1,0:T(8,128)(2,1)S(1)}, u32[]{:S(2)}) copy-start(bf16[32,2,256,128]{3,2,1,0:T(8,128)(2,1)S(1)} %shard_map.94.kv_ref) | copy-start | bytes 12582916
  80.4 2.2 %copy-start.2 = (bf16[2,4,4,2,256,128]{5,4,3,2,1,0:T(8,128)(2,1)S(1)}, bf16[2,4,4,2,256,128]{5,4,3,2,1,0:T(8,128)(2,1)}, u32[]{:S(2)}) copy-start(bf16[2,4,4,2,256,128]{5,4,3,2,1,0:T(8,128)(2,1)} %get-tuple-element.12.part) | copy-start | bytes 12582916

commit v2 on v0

v2 whole, which is shorter than its diff:
```python
import jax
import jax.numpy as jnp
from jax import lax
from jax.experimental import pallas as pl
from jax.experimental.pallas import tpu as pltpu
from jax.sharding import PartitionSpec as P
H = 128
G = 8
B = 128
NB = 24
NP = NB // 2
NBLK = 64
NK = 8
SC = H ** -0.5
C2 = SC * 1.4426950408889634
R = G * B
bf = jnp.bfloat16
f32 = jnp.float32
MESH = pl.DeviceIdType.MESH


def table_kernel(first, lists, counts, span, slots, used, index, inverse):
    def invert(s, _):
        inverse[span[s]] = s
        index[s] = 2 * NB
        index[NBLK + s] = 2 * NB
        return 0

    lax.fori_loop(0, NBLK, invert, 0, unroll=8)
    for j in range(2):
        pos = span[first[0] + j]
        n = counts[pos]


        def entry(e, _, j=j, pos=pos, n=n):
            s = inverse[lists[e, pos]]
            slots[j * NB + e] = s
            used[j * NB + e] = jnp.where(e < n, 1.0, 0.0)

            @pl.when(e < n)
            def _():
                index[j * NBLK + s] = j * NB + e
            return 0

        lax.fori_loop(0, NB, entry, 0, unroll=4)


def tables(key_lists, block_counts, span_table):
    sm = pl.BlockSpec(memory_space=pltpu.SMEM)
    i32 = jnp.int32
    first = (lax.axis_index("seq") * 2).astype(i32).reshape(1)
    return pl.pallas_call(
        table_kernel,
        out_shape=(jax.ShapeDtypeStruct((2 * NB,), i32), jax.ShapeDtypeStruct((2 * NB,), f32), jax.ShapeDtypeStruct((2 * NBLK,), i32)),
        in_specs=[sm] * 4,
        out_specs=[sm] * 3,
        scratch_shapes=[pltpu.SMEM((NBLK,), i32)],
    )(first, key_lists.T, block_counts, span_table)


def place():
    i = lax.axis_index("seq")
    j = lax.axis_index("kvh")
    return i, j, i // 8, (i // 2) % 4, i % 2


def seq_of(y, z, c):
    return (y * 4 + z) * 2 + c


def zrel(z):
    return [z, z + 1 - 2 * (z % 2), (z + 2) % 4, 3 - z]


ORDER = (1, 2, 3, 0)


def kernel(slots, used, index, k_hbm, v_hbm, q_hbm, do_hbm, dq_ref, ko_ref, vo_ref,
           kin, vin, q_ref, do_ref, tx, ka, va, part, qT, doT, qr, dor, e_buf, p_buf, pair_buf, dqT, racc, rinv, delta,
           rx0, acc, rxa, rxb, rxz, zown, res, rxh,
           s_in, hs, hr, gz_s, gz_r, gy_s, gy_r, gf_s, gf_r, gc_s, gc_r,
           s0, r0, sa, ra, sb, rb, sz, rz, sh, rh):
    i, j, y, z, c = place()
    zz = zrel(z)
    yy = [(y + 2) % 4, (y + 1) % 4, (y + 3) % 4, y]
    sib = (seq_of(y, z, 1 - c), j)
    up = (seq_of(yy[1], z, c), j)
    dn = (seq_of(yy[2], z, c), j)
    kva = (ka, va)
    sends = []

    def send(src, dst, ss, rs, dev):
        cp = pltpu.make_async_remote_copy(src_ref=src, dst_ref=dst, send_sem=ss, recv_sem=rs, device_id=dev, device_id_type=MESH)
        cp.start()
        sends.append(cp)
        return cp

    loads = [pltpu.make_async_copy(a, b, s_in.at[n]) for n, (a, b) in enumerate(((k_hbm, kin), (v_hbm, vin), (q_hbm, q_ref), (do_hbm, do_ref)))]
    for cp in loads:
        cp.start()
    barrier = pltpu.get_barrier_semaphore()
    near = [sib, up, dn] + [(seq_of(y, zz[r], c), j) for r in (1, 2, 3)]
    for dev in near + [(i, (j + d) % NK) for d in range(1, NK)]:
        pl.semaphore_signal(barrier, inc=1, device_id=dev, device_id_type=MESH)
    loads[0].wait()
    loads[1].wait()
    for h in range(NK):
        tx[h, 0] = kin[:, h * H:(h + 1) * H]
        tx[h, 1] = vin[:, h * H:(h + 1) * H]
    pl.semaphore_wait(barrier, len(near) + NK - 1)
    rows = pl.ds(pl.multiple_of((j % 4) * 32, 32), 32)
    heads = []
    for d in range(1, NK):
        h = (j + d) % NK
        for t in range(2):
            heads.append(send(tx.at[h, t], kva[t].at[2 * i + j // 4, rows, :], hs.at[t, d - 1], hr.at[t, d - 1], (i, h)))
    for t in range(2):
        kva[t][2 * i + j // 4, rows, :] = tx[j, t]

    def gather(t):
        def chunk(yp, r):
            return kva[t].at[pl.ds(2 * seq_of(yp, zz[r], c), 2)]

        def half(yp, r, p):
            return kva[t].at[2 * seq_of(yp, zz[r], c) + p]

        cs = []

        def to_sib(yp, r):
            n = len(cs)
            cs.append(send(chunk(yp, r), chunk(yp, r), gc_s.at[t, n], gc_r.at[t, n], sib))

        uc, dc, hu, hd, zc = [], [], [], [], []

        def around(r):
            uc.append(send(chunk(y, r), chunk(y, r), gy_s.at[t, 0, r], gy_r.at[t, 0, r], up))
            dc.append(send(chunk(y, r), chunk(y, r), gy_s.at[t, 1, r], gy_r.at[t, 1, r], dn))

        around(0)
        for r in (1, 2, 3):
            zc.append(send(chunk(y, 0), chunk(y, 0), gz_s.at[t, r - 1], gz_r.at[t, r - 1], (seq_of(y, zz[r], c), j)))
        to_sib(y, 0)
        yield
        for r in (1, 2, 3):
            zc[r - 1].wait_recv()
            around(r)
            to_sib(y, r)
        yield
        for r in range(4):
            uc[r].wait_recv()
            hu.append(send(half(yy[2], r, 0), half(yy[2], r, 0), gf_s.at[t, 0, r], gf_r.at[t, 0, r], up))
            to_sib(yy[2], r)
            dc[r].wait_recv()
            hd.append(send(half(yy[1], r, 1), half(yy[1], r, 1), gf_s.at[t, 1, r], gf_r.at[t, 1, r], dn))
            to_sib(yy[1], r)
            if r == 1:
                yield
        yield
        for r in range(4):
            hu[r].wait_recv()
            hd[r].wait_recv()
            to_sib(yy[0], r)
        yield
        for cp in cs:
            cp.wait_recv()

    def add(dst, a, b, *more):
        t = a.astype(f32) + b.astype(f32)
        for m in more:
            t = t + m.astype(f32)
        return t.astype(dst)

    def reduce(t, out_ref):
        mine = part.at[t, c]
        c0 = [send(part.at[t, 1 - c, yy[g]], rx0.at[t, g], s0.at[t, g], r0.at[t, g], sib) for g in range(4)]
        yield

        def base(g, r):
            acc[t, g, r] = add(bf, mine[yy[g], zz[r]], rx0[t, g, zz[r]])

        cu, cd, bu, bd, cz = [None] * 4, [None] * 4, {}, {}, [None] * 4
        c0[0].wait_recv()
        for r in ORDER:
            base(0, r)
            cu[r] = send(acc.at[t, 0, r, 0], rxa.at[t, 0, r], sa.at[t, 0, r], ra.at[t, 0, r], up)
            cd[r] = send(acc.at[t, 0, r, 1], rxa.at[t, 1, r], sa.at[t, 1, r], ra.at[t, 1, r], dn)
        yield
        c0[1].wait_recv()
        c0[2].wait_recv()
        for r in ORDER:
            base(1, r)
            bu[r, 1] = send(acc.at[t, 1, r, 1], rxb.at[t, 0, r, 1], sb.at[t, 0, r, 1], rb.at[t, 0, r, 1], up)
            base(2, r)
            bd[r, 0] = send(acc.at[t, 2, r, 0], rxb.at[t, 1, r, 0], sb.at[t, 1, r, 0], rb.at[t, 1, r, 0], dn)
        yield
        for r in ORDER:
            cu[r].wait_recv()
            acc[t, 1, r, 0] = add(bf, acc[t, 1, r, 0], rxa[t, 0, r])
            bu[r, 0] = send(acc.at[t, 1, r, 0], rxb.at[t, 0, r, 0], sb.at[t, 0, r, 0], rb.at[t, 0, r, 0], up)
            cd[r].wait_recv()
            acc[t, 2, r, 1] = add(bf, acc[t, 2, r, 1], rxa[t, 1, r])
            bd[r, 1] = send(acc.at[t, 2, r, 1], rxb.at[t, 1, r, 1], sb.at[t, 1, r, 1], rb.at[t, 1, r, 1], dn)
        yield
        c0[3].wait_recv()
        for r in ORDER:
            for p in range(2):
                bu[r, p].wait_recv()
                bd[r, p].wait_recv()
            if r:
                acc[t, 3, r] = add(bf, mine[y, zz[r]], rx0[t, 3, zz[r]], rxb[t, 0, r], rxb[t, 1, r])
                cz[r] = send(acc.at[t, 3, r], rxz.at[t, r - 1], sz.at[t, r - 1], rz.at[t, r - 1], (seq_of(y, zz[r], c), j))
            else:
                zown[t] = add(f32, mine[y, z], rx0[t, 3, z], rxb[t, 0, 0], rxb[t, 1, 0])
        yield
        for r in (1, 2, 3):
            cz[r].wait_recv()
        for h in range(NK):
            p, sl = h // 4, slice((h % 4) * 32, (h % 4) * 32 + 32)
            res[t, h] = add(bf, zown[t, p, sl, :], rxz[t, 0, p, sl, :], rxz[t, 1, p, sl, :], rxz[t, 2, p, sl, :])
        ch = []
        for d in range(1, NK):
            h = (j + d) % NK
            ch.append(send(res.at[t, h], rxh.at[t, NK - d], sh.at[t, d - 1], rh.at[t, d - 1], (i, h)))
        yield
        for d in range(NK):
            col = pl.ds(pl.multiple_of(((j + d) % NK) * H, H), H)
            if d == 0:
                out_ref[:, col] = res[t, j]
            else:
                ch[NK - d - 1].wait_recv()
                out_ref[:, col] = rxh[t, d]

    def advance(flow, n=1):
        for _ in range(n):
            next(flow, None)

    def prepare(b):
        for g in range(G):
            qb = q_ref[b * B:(b + 1) * B, g * H:(g + 1) * H]
            ob = do_ref[b * B:(b + 1) * B, g * H:(g + 1) * H]
            qr[b, g * B:(g + 1) * B, :] = qb
            dor[b, g * B:(g + 1) * B, :] = ob
            qT[b, :, g * B:(g + 1) * B] = qb.T
            doT[b, :, g * B:(g + 1) * B] = ob.T

    def two(t, b, n):
        got = []
        for p in range(2):
            got.append(kva[t][slots[b * NB + 2 * n + p]])
        return jnp.concatenate(got, 0)

    def loop(lo, hi, fn):
        def body(n, _):
            fn(n)
            return 0
        lax.fori_loop(lo, hi, body, 0)

    def scores(b, lo, hi):
        def one(n, first=False):
            s = jnp.dot(two(0, b, n), qT[b], preferred_element_type=f32)
            for p in range(2):
                x = jnp.exp2(s[p * B:(p + 1) * B] * C2)
                if first and p == 0:
                    key = lax.broadcasted_iota(jnp.int32, (B, R), 0)
                    qry = lax.broadcasted_iota(jnp.int32, (B, R), 1) % B
                    x = jnp.where(key <= qry, x, 0.0)
                e_buf[b, n, p * B:(p + 1) * B, :] = x
                t = jnp.sum(x.reshape(B // 8, 8, R), 0) * used[b * NB + 2 * n + p]
                if first and p == 0:
                    racc[b] = t
                else:
                    racc[b] += t
        if lo == 0:
            one(0, True)
            lo = 1
        loop(lo, hi, one)
        if hi == NP:
            rinv[b] = jnp.broadcast_to(1.0 / jnp.sum(racc[b], 0, keepdims=True), (8, R))

    def weights(b, n):
        return jnp.concatenate([e_buf[b, n, p * B:(p + 1) * B, :] * (rinv[b, 0:1, :] * used[b * NB + 2 * n + p]) for p in range(2)], 0)

    def values(b, lo, hi):
        def one(n):
            w = weights(b, n).astype(bf)
            o = jnp.dot(w, dor[b], preferred_element_type=f32)
            for p in range(2):
                pair_buf[b * NB + 2 * n + p] = o[p * B:(p + 1) * B]
        loop(lo, hi, one)

    def products(b, lo, hi):
        def one(n):
            p = jnp.dot(two(1, b, n), doT[b], preferred_element_type=f32)
            p_buf[n] = p
            for h in range(2):
                sl = slice(h * B, h * B + B)
                racc[b] += jnp.sum((e_buf[b, n, sl, :] * p[sl]).reshape(B // 8, 8, R), 0) * used[b * NB + 2 * n + h]
        if lo == 0:
            racc[b] = jnp.zeros((8, R), f32)
        loop(lo, hi, one)
        if hi == NP:
            delta[b] = jnp.broadcast_to(jnp.sum(racc[b], 0, keepdims=True) * rinv[b, 0:1, :], (8, R))
            dqT[...] = jnp.zeros_like(dqT)

    def grads(b, lo, hi):
        def one(n):
            w = weights(b, n)
            ds = (w * (p_buf[n] - delta[b, 0:1, :])).astype(bf)
            o = jnp.dot(ds, qr[b], preferred_element_type=f32)
            for p in range(2):
                pair_buf[b * NB + 2 * n + p] = o[p * B:(p + 1) * B]
            dqT[...] += lax.dot_general(two(0, b, n), ds, (((0,), (0,)), ((), ())), preferred_element_type=f32)
        loop(lo, hi, one)
        if hi == NP:
            for g in range(G):
                dq_ref[b * B:(b + 1) * B, g * H:(g + 1) * H] = (dqT[:, g * B:(g + 1) * B].T * SC).astype(bf)

    def collect(t, scale):
        def one(s):
            i_ = s // 2
            v = pair_buf[index[s]] + pair_buf[index[NBLK + s]]
            if scale != 1.0:
                v = v * scale
            part[t, i_ % 2, i_ // 8, (i_ // 2) % 4, s % 2] = v.astype(bf)
        loop(0, NBLK, one)

    pair_buf[2 * NB] = jnp.zeros((B, H), f32)
    loads[2].wait()
    loads[3].wait()
    prepare(0)
    for cp in heads:
        cp.wait_recv()
    kf, vf = gather(0), gather(1)
    advance(kf)
    prepare(1)
    advance(kf)
    advance(vf)
    advance(kf, 2)
    advance(vf)
    advance(kf, 2)
    scores(0, 0, 6)
    advance(vf)
    scores(0, 6, NP)
    advance(vf)
    values(0, 0, 6)
    advance(vf)
    values(0, 6, NP)
    scores(1, 0, NP)
    values(1, 0, NP)
    advance(vf)
    collect(1, 1.0)
    vr = reduce(1, vo_ref)
    advance(vr)
    products(0, 0, 6)
    advance(vr)
    products(0, 6, NP)
    advance(vr)
    grads(0, 0, 6)
    advance(vr)
    grads(0, 6, NP)
    products(1, 0, 6)
    advance(vr)
    products(1, 6, NP)
    grads(1, 0, 6)
    advance(vr)
    grads(1, 6, NP)
    collect(0, SC)
    kr = reduce(0, ko_ref)
    advance(kr, 2)
    advance(vr)
    for _ in kr:
        pass
    for cp in sends:
        cp.wait_send()


def fused(slots, used, index, k, v, q, do):
    vm = pl.BlockSpec(memory_space=pltpu.VMEM)
    sm = pl.BlockSpec(memory_space=pltpu.SMEM)
    hb = pl.BlockSpec(memory_space=pl.ANY)
    V = pltpu.VMEM
    D = pltpu.SemaphoreType.DMA
    tok = jax.ShapeDtypeStruct((32, NK * H), bf)
    return pl.pallas_call(
        kernel,
        out_shape=(jax.ShapeDtypeStruct((2 * B, R), bf), tok, tok),
        in_specs=[sm] * 3 + [hb] * 4,
        out_specs=[vm] * 3,
        scratch_shapes=[
            V((32, NK * H), bf), V((32, NK * H), bf), V((2 * B, R), bf), V((2 * B, R), bf),
            V((NK, 2, 32, H), bf), V((NBLK, B, H), bf), V((NBLK, B, H), bf), V((2, 2, 4, 4, 2, B, H), bf),
            V((2, H, R), bf), V((2, H, R), bf), V((2, R, H), bf), V((2, R, H), bf),
            V((2, NP, 2 * B, R), f32), V((NP, 2 * B, R), f32), V((2 * NB + 1, B, H), f32), V((H, R), f32),
            V((2, 8, R), f32), V((2, 8, R), f32), V((2, 8, R), f32),
            V((2, 4, 4, 2, B, H), bf), V((2, 4, 4, 2, B, H), bf), V((2, 2, 4, B, H), bf), V((2, 2, 4, 2, B, H), bf),
            V((2, 3, 2, B, H), bf), V((2, 2, B, H), f32), V((2, NK, 32, H), bf), V((2, NK, 32, H), bf),
            D((4,)), D((2, 7)), D((2, 7)), D((2, 3)), D((2, 3)), D((2, 2, 4)), D((2, 2, 4)), D((2, 2, 4)), D((2, 2, 4)), D((2, 16)), D((2, 16)),
            D((2, 4)), D((2, 4)), D((2, 2, 4)), D((2, 2, 4)), D((2, 2, 4, 2)), D((2, 2, 4, 2)), D((2, 3)), D((2, 3)), D((2, 7)), D((2, 7)),
        ],
        compiler_params=pltpu.CompilerParams(collective_id=0, has_side_effects=True, vmem_limit_bytes=62 << 20),
    )(slots, used, index, k, v, q, do)


def shards(queries, key_vector_rows, value_vector_rows, output_gradient, key_lists, block_counts, span_table):
    slots, used, index = tables(key_lists, block_counts, span_table)
    return fused(slots, used, index, key_vector_rows, value_vector_rows, queries, output_gradient)


def solution(mesh):
    tokens = P(("seq", "kvh"), None)
    heads = P("seq", "kvh")
    return jax.shard_map(
        shards,
        mesh=mesh,
        in_specs=(heads, tokens, tokens, heads, P(), P(), P()),
        out_specs=(heads, tokens, tokens),
        check_vma=False,
    )
```

time: 1240 us -> 112 us (0.09); the launches traced: 1220 us -> 111 us
  waiting for transfers between devices: 425 us -> 0 us
  loops' own time: 318 us -> 0 us
  matrix products: 193 us -> 0 us
  local copies, waits for them, and re-layouts: 159 us -> 3.4 us
  Pallas kernels: 0 us -> 106 us
  other arithmetic: 60 us -> 0 us
  blocking collectives: 33.5 us -> 0 us
  between operations: 17.8 us -> 0.66 us
    reduce_scatter x1 -> x0, waiting for transfers between devices: 318 us -> none  [shards(): kv_sums = lax.psum_scatter(buffer, 'seq', scatter_dimension=0, tiled=True)]
    another operation x4 -> x0, loops' own time: 318 us -> none  [the longest x2 160 us: shards(): lax.fori_loop(0, prepared_item[3], grad_maker(prepared_item), (zero_grad,...]
    dot_general x245 -> x0, matrix products: 193 us -> none  [the longest x70 72 us: block_scores(): jnp.einsum('tgd,sd->gts', query_blk, key_blk, preferred_element_type=jnp....]
    dynamic_slice x142 -> x0, local copies, waits for them, and re-layouts: 134 us -> none  [the longest x35 45.1 us: forward_step(): key_pos = key_lists[query_pos, entry_id]]
    pallas_call x0 -> x2, Pallas kernels: none -> 106 us  [the longest x1 105 us: fused(): pl.pallas_call(kernel, out_shape=(jax.ShapeDtypeStruct((2 * B, R), bf), t...]
    all_gather x2 -> x0, waiting for transfers between devices: 90.8 us -> none  [the longest x1 56.8 us: shards(): lax.all_gather(key_heads, 'seq', axis=0, tiled=True)]
    dynamic_update_slice x35 -> x0, other arithmetic: 56 us -> none  [grad_step(): lax.dynamic_update_slice_in_dim(buffer, previous + pair_kv, row_start, 0)]
    all_to_all x2 -> x0, blocking collectives: 33.5 us -> none  [the longest x1 20.2 us: shards(): lax.all_to_all(value_vector_rows, 'kvh', split_axis=1, concat_axis=0, til...]
  transfers between devices with their start and end apart: 5 -> 0, of which waited for: 5 -> 0; matrix products, arithmetic and copies ran while one was open for 1% -> 0% of each run, Pallas kernels for 0% -> 0%
where the time goes in v2:
time: 112 us; the launch traced here: 111 us
  Pallas kernels  106 us (95%)
  local copies, waits for them, and re-layouts  3.4 us (3%)
    pallas_call x1, Pallas kernels, fused(): pl.pallas_call(kernel, out_shape=(jax.ShapeDtypeStruct((2 * B, R), bf), t...  105 us
    unnamed x7, local copies, waits for them, and re-layouts  3.4 us

profile of v2, /device:TPU:2, one launch (start us, length us, event | category | flops | bytes accessed | tf_op | source)
XLA Modules:
  0.0 110.5 jit_solution(2126637656285313551)
XLA Ops:
  0.6 1.8 %shard_map.94 = (s32[48]{0:T(128)}, f32[48]{0:T(128)}, s32[128]{0:T(128)}) custom-call(s32[1]{0:T(128)} %bitcast.first, s32[24,64]{1,0:T(8,128)} %bitcast.2, s32[64]{0:T(128)} %counts.1, s32[64]{0:T(128)} %span.1), custom_call_target="tpu_custom_call" | custom-call | tf_op jit(solution)/shard_map/pallas_call | solution.py:52
  2.5 104.6 %shard_map.95 = (bf16[256,1024]{1,0:T(8,128)(2,1)}, bf16[32,1024]{1,0:T(8,128)(2,1)}, bf16[32,1024]{1,0:T(8,128)(2,1)}) custom-call(s32[48]{0:T(128)} %get-tuple-element.6.slots, f32[48]{0:T(128)} %get-tuple-element.7.used, s32[128]{0:T(128)} %get-tuple-element.8.index, bf16[32,1024]{1,0:T(8,128)(2,1)} %k_hbm.1, bf16[32,1024]{1,0:T(8,128)(2,1)} %v_hbm.1, ...), custom_call_target="tpu_custom_call" | custom-call | tf_op jit(solution)/shard_map/pallas_call | solution.py:384
  107.1 0.0 copy-start.1
  107.1 1.9 %copy.13 = bf16[256,1024]{1,0:T(8,128)(2,1)} copy(bf16[256,1024]{1,0:T(8,128)(2,1)} %get-tuple-element.12) | data formatting | bytes 1048576
  109.0 0.0 copy-done.1
  109.0 0.0 copy-start
  109.0 0.6 copy.14
  109.6 0.2 copy-done
  109.9 0.6 copy.15
Async XLA Ops:
  107.1 1.9 %copy-start.1 = (bf16[32,1024]{1,0:T(8,128)(2,1)S(1)}, bf16[32,1024]{1,0:T(8,128)(2,1)}, u32[]{:S(2)}) copy-start(bf16[32,1024]{1,0:T(8,128)(2,1)} %get-tuple-element.13) | copy-start | bytes 196612
  109.0 0.9 copy-start

commit v3 on v2

--- a/solution.py
+++ b/solution.py
@@ -17,6 +17,7 @@
 bf = jnp.bfloat16
 f32 = jnp.float32
 MESH = pl.DeviceIdType.MESH
+UNROLL = 3
 
 
 def table_kernel(first, lists, counts, span, slots, used, index, inverse):
@@ -77,9 +78,9 @@
 
 def kernel(slots, used, index, k_hbm, v_hbm, q_hbm, do_hbm, dq_ref, ko_ref, vo_ref,
            kin, vin, q_ref, do_ref, tx, ka, va, part, qT, doT, qr, dor, e_buf, p_buf, pair_buf, dqT, racc, rinv, delta,
-           rx0, acc, rxa, rxb, rxz, zown, res, rxh,
+           rx0, acc, rxb, rxz, zown, res, rxh,
            s_in, hs, hr, gz_s, gz_r, gy_s, gy_r, gf_s, gf_r, gc_s, gc_r,
-           s0, r0, sa, ra, sb, rb, sz, rz, sh, rh):
+           s0, r0, sb, rb, sz, rz, sh, rh):
     i, j, y, z, c = place()
     zz = zrel(z)
     yy = [(y + 2) % 4, (y + 1) % 4, (y + 3) % 4, y]
@@ -99,7 +100,7 @@
     for cp in loads:
         cp.start()
     barrier = pltpu.get_barrier_semaphore()
-    near = [sib, up, dn] + [(seq_of(y, zz[r], c), j) for r in (1, 2, 3)]
+    near = [sib, up, dn, (seq_of(yy[0], z, c), j)] + [(seq_of(y, zz[r], c), j) for r in (1, 2, 3)]
     for dev in near + [(i, (j + d) % NK) for d in range(1, NK)]:
         pl.semaphore_signal(barrier, inc=1, device_id=dev, device_id_type=MESH)
     loads[0].wait()
@@ -136,11 +137,14 @@
             uc.append(send(chunk(y, r), chunk(y, r), gy_s.at[t, 0, r], gy_r.at[t, 0, r], up))
             dc.append(send(chunk(y, r), chunk(y, r), gy_s.at[t, 1, r], gy_r.at[t, 1, r], dn))
 
-        around(0)
+        if t == 0:
+            around(0)
         for r in (1, 2, 3):
             zc.append(send(chunk(y, 0), chunk(y, 0), gz_s.at[t, r - 1], gz_r.at[t, r - 1], (seq_of(y, zz[r], c), j)))
         to_sib(y, 0)
         yield
+        if t == 1:
+            around(0)
         for r in (1, 2, 3):
             zc[r - 1].wait_recv()
             around(r)
@@ -172,45 +176,26 @@
 
     def reduce(t, out_ref):
         mine = part.at[t, c]
-        c0 = [send(part.at[t, 1 - c, yy[g]], rx0.at[t, g], s0.at[t, g], r0.at[t, g], sib) for g in range(4)]
-        yield
-
-        def base(g, r):
-            acc[t, g, r] = add(bf, mine[yy[g], zz[r]], rx0[t, g, zz[r]])
-
-        cu, cd, bu, bd, cz = [None] * 4, [None] * 4, {}, {}, [None] * 4
-        c0[0].wait_recv()
+        c0, cb, cz = [None] * 4, {}, [None] * 4
         for r in ORDER:
-            base(0, r)
-            cu[r] = send(acc.at[t, 0, r, 0], rxa.at[t, 0, r], sa.at[t, 0, r], ra.at[t, 0, r], up)
-            cd[r] = send(acc.at[t, 0, r, 1], rxa.at[t, 1, r], sa.at[t, 1, r], ra.at[t, 1, r], dn)
-        yield
-        c0[1].wait_recv()
-        c0[2].wait_recv()
+            c0[r] = send(part.at[t, 1 - c, :, zz[r]], rx0.at[t, r], s0.at[t, r], r0.at[t, r], sib)
+        yield
         for r in ORDER:
-            base(1, r)
-            bu[r, 1] = send(acc.at[t, 1, r, 1], rxb.at[t, 0, r, 1], sb.at[t, 0, r, 1], rb.at[t, 0, r, 1], up)
-            base(2, r)
-            bd[r, 0] = send(acc.at[t, 2, r, 0], rxb.at[t, 1, r, 0], sb.at[t, 1, r, 0], rb.at[t, 1, r, 0], dn)
+            c0[r].wait_recv()
+            for g in range(3):
+                acc[t, g, r] = add(bf, mine[yy[g], zz[r]], rx0[t, r, yy[g]])
+                cb[g, r] = send(acc.at[t, g, r], rxb.at[t, g, r], sb.at[t, g, r], rb.at[t, g, r], (seq_of(yy[g], z, c), j))
         yield
         for r in ORDER:
-            cu[r].wait_recv()
-            acc[t, 1, r, 0] = add(bf, acc[t, 1, r, 0], rxa[t, 0, r])
-            bu[r, 0] = send(acc.at[t, 1, r, 0], rxb.at[t, 0, r, 0], sb.at[t, 0, r, 0], rb.at[t, 0, r, 0], up)
-            cd[r].wait_recv()
-            acc[t, 2, r, 1] = add(bf, acc[t, 2, r, 1], rxa[t, 1, r])
-            bd[r, 1] = send(acc.at[t, 2, r, 1], rxb.at[t, 1, r, 1], sb.at[t, 1, r, 1], rb.at[t, 1, r, 1], dn)
-        yield
-        c0[3].wait_recv()
-        for r in ORDER:
-            for p in range(2):
-                bu[r, p].wait_recv()
-                bd[r, p].wait_recv()
+            for g in range(3):
+                cb[g, r].wait_recv()
             if r:
-                acc[t, 3, r] = add(bf, mine[y, zz[r]], rx0[t, 3, zz[r]], rxb[t, 0, r], rxb[t, 1, r])
+                acc[t, 3, r] = add(bf, mine[y, zz[r]], rx0[t, r, y], rxb[t, 0, r], rxb[t, 1, r], rxb[t, 2, r])
                 cz[r] = send(acc.at[t, 3, r], rxz.at[t, r - 1], sz.at[t, r - 1], rz.at[t, r - 1], (seq_of(y, zz[r], c), j))
+                if r == 2:
+                    yield
             else:
-                zown[t] = add(f32, mine[y, z], rx0[t, 3, z], rxb[t, 0, 0], rxb[t, 1, 0])
+                zown[t] = add(f32, mine[y, z], rx0[t, 0, y], rxb[t, 0, 0], rxb[t, 1, 0], rxb[t, 2, 0])
         yield
         for r in (1, 2, 3):
             cz[r].wait_recv()
@@ -249,11 +234,11 @@
             got.append(kva[t][slots[b * NB + 2 * n + p]])
         return jnp.concatenate(got, 0)
 
-    def loop(lo, hi, fn):
+    def loop(lo, hi, fn, unroll=UNROLL):
         def body(n, _):
             fn(n)
             return 0
-        lax.fori_loop(lo, hi, body, 0)
+        lax.fori_loop(lo, hi, body, 0, unroll=unroll)
 
     def scores(b, lo, hi):
         def one(n, first=False):
@@ -300,7 +285,6 @@
         loop(lo, hi, one)
         if hi == NP:
             delta[b] = jnp.broadcast_to(jnp.sum(racc[b], 0, keepdims=True) * rinv[b, 0:1, :], (8, R))
-            dqT[...] = jnp.zeros_like(dqT)
 
     def grads(b, lo, hi):
         def one(n):
@@ -309,7 +293,14 @@
             o = jnp.dot(ds, qr[b], preferred_element_type=f32)
             for p in range(2):
                 pair_buf[b * NB + 2 * n + p] = o[p * B:(p + 1) * B]
-            dqT[...] += lax.dot_general(two(0, b, n), ds, (((0,), (0,)), ((), ())), preferred_element_type=f32)
+            e_buf[b, n] = ds.astype(f32)
+        loop(lo, hi, one)
+
+    def queries(b, lo, hi):
+        def one(n):
+            dqT[...] += lax.dot_general(two(0, b, n), e_buf[b, n].astype(bf), (((0,), (0,)), ((), ())), preferred_element_type=f32)
+        if lo == 0:
+            dqT[...] = jnp.zeros_like(dqT)
         loop(lo, hi, one)
         if hi == NP:
             for g in range(G):
@@ -338,37 +329,36 @@
     advance(kf, 2)
     advance(vf)
     advance(kf, 2)
-    scores(0, 0, 6)
-    advance(vf)
-    scores(0, 6, NP)
-    advance(vf)
-    values(0, 0, 6)
-    advance(vf)
-    values(0, 6, NP)
+    scores(0, 0, NP)
+    advance(vf)
+    values(0, 0, NP)
+    advance(vf)
     scores(1, 0, NP)
+    advance(vf)
     values(1, 0, NP)
-    advance(vf)
     collect(1, 1.0)
     vr = reduce(1, vo_ref)
     advance(vr)
-    products(0, 0, 6)
-    advance(vr)
-    products(0, 6, NP)
-    advance(vr)
-    grads(0, 0, 6)
-    advance(vr)
-    grads(0, 6, NP)
-    products(1, 0, 6)
-    advance(vr)
-    products(1, 6, NP)
-    grads(1, 0, 6)
-    advance(vr)
-    grads(1, 6, NP)
+    advance(vf)
+    products(0, 0, NP)
+    advance(vr)
+    grads(0, 0, NP)
+    products(1, 0, NP)
+    grads(1, 0, NP)
     collect(0, SC)
     kr = reduce(0, ko_ref)
+    advance(kr)
+    advance(vr)
+    queries(0, 0, NP)
+    advance(kr)
+    advance(vr)
+    queries(1, 0, NP)
+    advance(vr)
     advance(kr, 2)
     advance(vr)
     for _ in kr:
+        pass
+    for _ in vr:
         pass
     for cp in sends:
         cp.wait_send()
@@ -392,10 +382,10 @@
             V((2, H, R), bf), V((2, H, R), bf), V((2, R, H), bf), V((2, R, H), bf),
             V((2, NP, 2 * B, R), f32), V((NP, 2 * B, R), f32), V((2 * NB + 1, B, H), f32), V((H, R), f32),
             V((2, 8, R), f32), V((2, 8, R), f32), V((2, 8, R), f32),
-            V((2, 4, 4, 2, B, H), bf), V((2, 4, 4, 2, B, H), bf), V((2, 2, 4, B, H), bf), V((2, 2, 4, 2, B, H), bf),
+            V((2, 4, 4, 2, B, H), bf), V((2, 4, 4, 2, B, H), bf), V((2, 3, 4, 2, B, H), bf),
             V((2, 3, 2, B, H), bf), V((2, 2, B, H), f32), V((2, NK, 32, H), bf), V((2, NK, 32, H), bf),
             D((4,)), D((2, 7)), D((2, 7)), D((2, 3)), D((2, 3)), D((2, 2, 4)), D((2, 2, 4)), D((2, 2, 4)), D((2, 2, 4)), D((2, 16)), D((2, 16)),
-            D((2, 4)), D((2, 4)), D((2, 2, 4)), D((2, 2, 4)), D((2, 2, 4, 2)), D((2, 2, 4, 2)), D((2, 3)), D((2, 3)), D((2, 7)), D((2, 7)),
+            D((2, 4)), D((2, 4)), D((2, 3, 4)), D((2, 3, 4)), D((2, 3)), D((2, 3)), D((2, 7)), D((2, 7)),
         ],
         compiler_params=pltpu.CompilerParams(collective_id=0, has_side_effects=True, vmem_limit_bytes=62 << 20),
     )(slots, used, index, k, v, q, do)

time: 112 us -> 92 us (0.82)
  Pallas kernels: 106 us -> 87.5 us
    pallas_call x1, Pallas kernels: 105 us -> 85.6 us  [fused(): pl.pallas_call(kernel, out_shape=(jax.ShapeDtypeStruct((2 * B, R), bf), t...]
where the time goes in v3:
time: 92 us; the launch traced here: 91.5 us
  Pallas kernels  87.5 us (95%)
  local copies, waits for them, and re-layouts  3.4 us (4%)
    pallas_call x1, Pallas kernels, fused(): pl.pallas_call(kernel, out_shape=(jax.ShapeDtypeStruct((2 * B, R), bf), t...  85.6 us
    unnamed x7, local copies, waits for them, and re-layouts  3.4 us
    pallas_call x1, Pallas kernels, tables(): pl.pallas_call(table_kernel, out_shape=(jax.ShapeDtypeStruct((2 * NB,), i...  1.85 us

profile of v3, /device:TPU:2, one launch (start us, length us, event | category | flops | bytes accessed | tf_op | source)
XLA Modules:
  0.0 91.5 jit_solution(2095728168573923941)
XLA Ops:
  0.6 1.8 %shard_map.94 = (s32[48]{0:T(128)}, f32[48]{0:T(128)}, s32[128]{0:T(128)}) custom-call(s32[1]{0:T(128)} %bitcast.first, s32[24,64]{1,0:T(8,128)} %bitcast.2, s32[64]{0:T(128)} %counts.1, s32[64]{0:T(128)} %span.1), custom_call_target="tpu_custom_call" | custom-call | tf_op jit(solution)/shard_map/pallas_call | solution.py:53
  2.5 85.6 %shard_map.95 = (bf16[256,1024]{1,0:T(8,128)(2,1)}, bf16[32,1024]{1,0:T(8,128)(2,1)}, bf16[32,1024]{1,0:T(8,128)(2,1)}) custom-call(s32[48]{0:T(128)} %get-tuple-element.6.slots, f32[48]{0:T(128)} %get-tuple-element.7.used, s32[128]{0:T(128)} %get-tuple-element.8.index, bf16[32,1024]{1,0:T(8,128)(2,1)} %k_hbm.1, bf16[32,1024]{1,0:T(8,128)(2,1)} %v_hbm.1, ...), custom_call_target="tpu_custom_call" | custom-call | tf_op jit(solution)/shard_map/pallas_call | solution.py:374
  88.1 0.0 copy-start.1
  88.1 1.9 %copy.13 = bf16[256,1024]{1,0:T(8,128)(2,1)} copy(bf16[256,1024]{1,0:T(8,128)(2,1)} %get-tuple-element.12) | data formatting | bytes 1048576
  90.0 0.0 copy-done.1
  90.0 0.0 copy-start
  90.0 0.6 copy.14
  90.6 0.2 copy-done
  90.9 0.6 copy.15
Async XLA Ops:
  88.1 1.9 %copy-start.1 = (bf16[32,1024]{1,0:T(8,128)(2,1)S(1)}, bf16[32,1024]{1,0:T(8,128)(2,1)}, u32[]{:S(2)}) copy-start(bf16[32,1024]{1,0:T(8,128)(2,1)} %get-tuple-element.13) | copy-start | bytes 196612
  90.0 0.9 copy-start

commit v4 on v3

--- a/solution.py
+++ b/solution.py
@@ -20,45 +20,6 @@
 UNROLL = 3
 
 
-def table_kernel(first, lists, counts, span, slots, used, index, inverse):
-    def invert(s, _):
-        inverse[span[s]] = s
-        index[s] = 2 * NB
-        index[NBLK + s] = 2 * NB
-        return 0
-
-    lax.fori_loop(0, NBLK, invert, 0, unroll=8)
-    for j in range(2):
-        pos = span[first[0] + j]
-        n = counts[pos]
-
-
-        def entry(e, _, j=j, pos=pos, n=n):
-            s = inverse[lists[e, pos]]
-            slots[j * NB + e] = s
-            used[j * NB + e] = jnp.where(e < n, 1.0, 0.0)
-
-            @pl.when(e < n)
-            def _():
-                index[j * NBLK + s] = j * NB + e
-            return 0
-
-        lax.fori_loop(0, NB, entry, 0, unroll=4)
-
-
-def tables(key_lists, block_counts, span_table):
-    sm = pl.BlockSpec(memory_space=pltpu.SMEM)
-    i32 = jnp.int32
-    first = (lax.axis_index("seq") * 2).astype(i32).reshape(1)
-    return pl.pallas_call(
-        table_kernel,
-        out_shape=(jax.ShapeDtypeStruct((2 * NB,), i32), jax.ShapeDtypeStruct((2 * NB,), f32), jax.ShapeDtypeStruct((2 * NBLK,), i32)),
-        in_specs=[sm] * 4,
-        out_specs=[sm] * 3,
-        scratch_shapes=[pltpu.SMEM((NBLK,), i32)],
-    )(first, key_lists.T, block_counts, span_table)
-
-
 def place():
     i = lax.axis_index("seq")
     j = lax.axis_index("kvh")
@@ -76,8 +37,8 @@
 ORDER = (1, 2, 3, 0)
 
 
-def kernel(slots, used, index, k_hbm, v_hbm, q_hbm, do_hbm, dq_ref, ko_ref, vo_ref,
-           kin, vin, q_ref, do_ref, tx, ka, va, part, qT, doT, qr, dor, e_buf, p_buf, pair_buf, dqT, racc, rinv, delta,
+def kernel(lists_hbm, counts_hbm, span_hbm, row_hbm, k_hbm, v_hbm, q_hbm, do_hbm, dq_ref, ko_ref, vo_ref,
+           lists, counts, span, row, tab_v, tab, kin, vin, q_ref, do_ref, tx, ka, va, part, qT, doT, qr, dor, e_buf, p_buf, pair_buf, dqT, racc, rinv, delta,
            rx0, acc, rxb, rxz, zown, res, rxh,
            s_in, hs, hr, gz_s, gz_r, gy_s, gy_r, gf_s, gf_r, gc_s, gc_r,
            s0, r0, sb, rb, sz, rz, sh, rh):
@@ -96,13 +57,13 @@
         sends.append(cp)
         return cp
 
-    loads = [pltpu.make_async_copy(a, b, s_in.at[n]) for n, (a, b) in enumerate(((k_hbm, kin), (v_hbm, vin), (q_hbm, q_ref), (do_hbm, do_ref)))]
-    for cp in loads:
-        cp.start()
     barrier = pltpu.get_barrier_semaphore()
     near = [sib, up, dn, (seq_of(yy[0], z, c), j)] + [(seq_of(y, zz[r], c), j) for r in (1, 2, 3)]
     for dev in near + [(i, (j + d) % NK) for d in range(1, NK)]:
         pl.semaphore_signal(barrier, inc=1, device_id=dev, device_id_type=MESH)
+    loads = [pltpu.make_async_copy(a, b, s_in.at[n]) for n, (a, b) in enumerate(((k_hbm, kin), (v_hbm, vin), (q_hbm, q_ref), (do_hbm, do_ref), (lists_hbm, lists), (counts_hbm, counts), (span_hbm, span), (row_hbm, row)))]
+    for cp in loads:
+        cp.start()
     loads[0].wait()
     loads[1].wait()
     for h in range(NK):
@@ -178,7 +139,10 @@
         mine = part.at[t, c]
         c0, cb, cz = [None] * 4, {}, [None] * 4
         for r in ORDER:
+            collect(t, 1 - c, r)
             c0[r] = send(part.at[t, 1 - c, :, zz[r]], rx0.at[t, r], s0.at[t, r], r0.at[t, r], sib)
+        for r in ORDER:
+            collect(t, c, r)
         yield
         for r in ORDER:
             c0[r].wait_recv()
@@ -231,7 +195,7 @@
     def two(t, b, n):
         got = []
         for p in range(2):
-            got.append(kva[t][slots[b * NB + 2 * n + p]])
+            got.append(kva[t][tab[2 * n + p, b]])
         return jnp.concatenate(got, 0)
 
     def loop(lo, hi, fn, unroll=UNROLL):
@@ -250,7 +214,7 @@
                     qry = lax.broadcasted_iota(jnp.int32, (B, R), 1) % B
                     x = jnp.where(key <= qry, x, 0.0)
                 e_buf[b, n, p * B:(p + 1) * B, :] = x
-                t = jnp.sum(x.reshape(B // 8, 8, R), 0) * used[b * NB + 2 * n + p]
+                t = jnp.sum(x.reshape(B // 8, 8, R), 0) * tab[2 * n + p, 2 + b].astype(f32)
                 if first and p == 0:
                     racc[b] = t
                 else:
@@ -263,12 +227,13 @@
             rinv[b] = jnp.broadcast_to(1.0 / jnp.sum(racc[b], 0, keepdims=True), (8, R))
 
     def weights(b, n):
-        return jnp.concatenate([e_buf[b, n, p * B:(p + 1) * B, :] * (rinv[b, 0:1, :] * used[b * NB + 2 * n + p]) for p in range(2)], 0)
+        return jnp.concatenate([e_buf[b, n, p * B:(p + 1) * B, :] * (rinv[b, 0:1, :] * tab[2 * n + p, 2 + b].astype(f32)) for p in range(2)], 0)
 
     def values(b, lo, hi):
         def one(n):
-            w = weights(b, n).astype(bf)
-            o = jnp.dot(w, dor[b], preferred_element_type=f32)
+            w = weights(b, n)
+            e_buf[b, n] = w
+            o = jnp.dot(w.astype(bf), dor[b], preferred_element_type=f32)
             for p in range(2):
                 pair_buf[b * NB + 2 * n + p] = o[p * B:(p + 1) * B]
         loop(lo, hi, one)
@@ -277,19 +242,16 @@
         def one(n):
             p = jnp.dot(two(1, b, n), doT[b], preferred_element_type=f32)
             p_buf[n] = p
-            for h in range(2):
-                sl = slice(h * B, h * B + B)
-                racc[b] += jnp.sum((e_buf[b, n, sl, :] * p[sl]).reshape(B // 8, 8, R), 0) * used[b * NB + 2 * n + h]
+            racc[b] += jnp.sum((e_buf[b, n] * p).reshape(2 * B // 8, 8, R), 0)
         if lo == 0:
             racc[b] = jnp.zeros((8, R), f32)
         loop(lo, hi, one)
         if hi == NP:
-            delta[b] = jnp.broadcast_to(jnp.sum(racc[b], 0, keepdims=True) * rinv[b, 0:1, :], (8, R))
+            delta[b] = jnp.broadcast_to(jnp.sum(racc[b], 0, keepdims=True), (8, R))
 
     def grads(b, lo, hi):
         def one(n):
-            w = weights(b, n)
-            ds = (w * (p_buf[n] - delta[b, 0:1, :])).astype(bf)
+            ds = (e_buf[b, n] * (p_buf[n] - delta[b, 0:1, :])).astype(bf)
             o = jnp.dot(ds, qr[b], preferred_element_type=f32)
             for p in range(2):
                 pair_buf[b * NB + 2 * n + p] = o[p * B:(p + 1) * B]
@@ -306,14 +268,13 @@
             for g in range(G):
                 dq_ref[b * B:(b + 1) * B, g * H:(g + 1) * H] = (dqT[:, g * B:(g + 1) * B].T * SC).astype(bf)
 
-    def collect(t, scale):
-        def one(s):
-            i_ = s // 2
-            v = pair_buf[index[s]] + pair_buf[index[NBLK + s]]
-            if scale != 1.0:
-                v = v * scale
-            part[t, i_ % 2, i_ // 8, (i_ // 2) % 4, s % 2] = v.astype(bf)
-        loop(0, NBLK, one)
+    def collect(t, core, r):
+        def one(m):
+            yp, p = m // 2, m % 2
+            k = 2 * seq_of(yp, zz[r], core) + p
+            v = pair_buf[tab[NB, k]] + pair_buf[tab[NB + 1, k]]
+            part[t, core, yp, zz[r], p] = (v if t else v * SC).astype(bf)
+        loop(0, 8, one, 4)
 
     pair_buf[2 * NB] = jnp.zeros((B, H), f32)
     loads[2].wait()
@@ -324,6 +285,25 @@
     kf, vf = gather(0), gather(1)
     advance(kf)
     prepare(1)
+    for cp in loads[4:]:
+        cp.wait()
+    lane = lax.broadcasted_iota(jnp.int32, (NB, NBLK), 1)
+    entry = lax.broadcasted_iota(jnp.int32, (NB, NBLK), 0)
+    wide = lax.broadcasted_iota(jnp.int32, (NB, H), 1)
+    mixed = jnp.zeros((NB, H), jnp.int32)
+    for b in range(2):
+        pos = span[2 * i + b]
+        col = jnp.sum(jnp.where(lane == pos, lists[...], 0), 1, keepdims=True)
+        hit = row[...] == col
+        mixed = jnp.where(wide == b, jnp.min(jnp.where(hit, lane, NBLK - 1), 1, keepdims=True), mixed)
+        valid = entry < counts[pos]
+        mixed = jnp.where(jnp.logical_and(wide == 2 + b, lax.broadcasted_iota(jnp.int32, (NB, H), 0) < counts[pos]), 1, mixed)
+        at = jnp.where(jnp.logical_and(hit, valid), entry + b * NB, 2 * NB)
+        tab_v[NB + b:NB + b + 1, 0:NBLK] = jnp.min(at, 0, keepdims=True)
+    tab_v[0:NB, :] = mixed
+    to_scalar = pltpu.make_async_copy(tab_v, tab, s_in.at[8])
+    to_scalar.start()
+    to_scalar.wait()
     advance(kf)
     advance(vf)
     advance(kf, 2)
@@ -336,7 +316,6 @@
     scores(1, 0, NP)
     advance(vf)
     values(1, 0, NP)
-    collect(1, 1.0)
     vr = reduce(1, vo_ref)
     advance(vr)
     advance(vf)
@@ -345,7 +324,6 @@
     grads(0, 0, NP)
     products(1, 0, NP)
     grads(1, 0, NP)
-    collect(0, SC)
     kr = reduce(0, ko_ref)
     advance(kr)
     advance(vr)
@@ -364,9 +342,18 @@
         cp.wait_send()
 
 
-def fused(slots, used, index, k, v, q, do):
+def finish_kernel(a, b, c, ao, bo, co):
+    ao[...] = a[...]
+    bo[...] = b[...]
+    co[...] = c[...]
+
+
+def finish(*outs):
+    return pl.pallas_call(finish_kernel, out_shape=tuple(jax.ShapeDtypeStruct(o.shape, o.dtype) for o in outs))(*outs)
+
+
+def fused(lists, counts, span, row, k, v, q, do):
     vm = pl.BlockSpec(memory_space=pltpu.VMEM)
-    sm = pl.BlockSpec(memory_space=pltpu.SMEM)
     hb = pl.BlockSpec(memory_space=pl.ANY)
     V = pltpu.VMEM
     D = pltpu.SemaphoreType.DMA
@@ -374,9 +361,11 @@
     return pl.pallas_call(
         kernel,
         out_shape=(jax.ShapeDtypeStruct((2 * B, R), bf), tok, tok),
-        in_specs=[sm] * 3 + [hb] * 4,
+        in_specs=[hb] * 8,
         out_specs=[vm] * 3,
         scratch_shapes=[
+            V((NB, NBLK), jnp.int32), pltpu.SMEM((NBLK,), jnp.int32), pltpu.SMEM((NBLK,), jnp.int32), V((1, NBLK), jnp.int32),
+            V((NB + 8, H), jnp.int32), pltpu.SMEM((NB + 8, H), jnp.int32),
             V((32, NK * H), bf), V((32, NK * H), bf), V((2 * B, R), bf), V((2 * B, R), bf),
             V((NK, 2, 32, H), bf), V((NBLK, B, H), bf), V((NBLK, B, H), bf), V((2, 2, 4, 4, 2, B, H), bf),
             V((2, H, R), bf), V((2, H, R), bf), V((2, R, H), bf), V((2, R, H), bf),
@@ -384,16 +373,15 @@
             V((2, 8, R), f32), V((2, 8, R), f32), V((2, 8, R), f32),
             V((2, 4, 4, 2, B, H), bf), V((2, 4, 4, 2, B, H), bf), V((2, 3, 4, 2, B, H), bf),
             V((2, 3, 2, B, H), bf), V((2, 2, B, H), f32), V((2, NK, 32, H), bf), V((2, NK, 32, H), bf),
-            D((4,)), D((2, 7)), D((2, 7)), D((2, 3)), D((2, 3)), D((2, 2, 4)), D((2, 2, 4)), D((2, 2, 4)), D((2, 2, 4)), D((2, 16)), D((2, 16)),
+            D((9,)), D((2, 7)), D((2, 7)), D((2, 3)), D((2, 3)), D((2, 2, 4)), D((2, 2, 4)), D((2, 2, 4)), D((2, 2, 4)), D((2, 16)), D((2, 16)),
             D((2, 4)), D((2, 4)), D((2, 3, 4)), D((2, 3, 4)), D((2, 3)), D((2, 3)), D((2, 7)), D((2, 7)),
         ],
         compiler_params=pltpu.CompilerParams(collective_id=0, has_side_effects=True, vmem_limit_bytes=62 << 20),
-    )(slots, used, index, k, v, q, do)
+    )(lists, counts, span, row, k, v, q, do)
 
 
 def shards(queries, key_vector_rows, value_vector_rows, output_gradient, key_lists, block_counts, span_table):
-    slots, used, index = tables(key_lists, block_counts, span_table)
-    return fused(slots, used, index, key_vector_rows, value_vector_rows, queries, output_gradient)
+    return finish(*fused(key_lists.T, block_counts, span_table, span_table.reshape(1, NBLK), key_vector_rows, value_vector_rows, queries, output_gradient))
 
 
 def solution(mesh):

time: 92 us -> 87.6 us (0.952)
  local copies, waits for them, and re-layouts: 3.4 us -> 0 us
  Pallas kernels: 87.5 us -> 86.1 us
    unnamed x7 -> x0, local copies, waits for them, and re-layouts: 3.4 us -> none
    pallas_call x1, Pallas kernels: 85.6 us -> 84.2 us  [fused(): pl.pallas_call(kernel, out_shape=(jax.ShapeDtypeStruct((2 * B, R), bf), t...]
where the time goes in v4:
time: 87.6 us; the launch traced here: 86.8 us
  Pallas kernels  86.1 us (98%)
    pallas_call x1, Pallas kernels, fused(): pl.pallas_call(kernel, out_shape=(jax.ShapeDtypeStruct((2 * B, R), bf), t...  84.2 us
    pallas_call x1, Pallas kernels, finish(): pl.pallas_call(finish_kernel, out_shape=tuple((jax.ShapeDtypeStruct(o.sha...  1.93 us

profile of v4, /device:TPU:2, one launch (start us, length us, event | category | flops | bytes accessed | tf_op | source)
XLA Modules:
  0.0 86.8 jit_solution(2157953067848847940)
XLA Ops:
  0.6 84.2 %shard_map.94 = (bf16[256,1024]{1,0:T(8,128)(2,1)}, bf16[32,1024]{1,0:T(8,128)(2,1)}, bf16[32,1024]{1,0:T(8,128)(2,1)}) custom-call(s32[24,64]{1,0:T(8,128)} %bitcast.2, s32[64]{0:T(128)} %counts_hbm.1, s32[64]{0:T(128)} %span_hbm.1, s32[1,64]{1,0:T(1,128)} %bitcast.3, bf16[32,1024]{1,0:T(8,128)(2,1)} %k_hbm.1, bf16[32,1024]{1,0:T(8,128)(2,1)} %v_hbm.1, ...), custom_call_target="tpu_custom_call" | custom-call | tf_op jit(solution)/shard_map/pallas_call | solution.py:361
  84.9 1.9 %shard_map.95 = (bf16[256,1024]{1,0:T(8,128)(2,1)}, bf16[32,1024]{1,0:T(8,128)(2,1)}, bf16[32,1024]{1,0:T(8,128)(2,1)}) custom-call(bf16[256,1024]{1,0:T(8,128)(2,1)} %get-tuple-element.6.a, bf16[32,1024]{1,0:T(8,128)(2,1)} %get-tuple-element.7.b, bf16[32,1024]{1,0:T(8,128)(2,1)} %get-tuple-element.8.c), custom_call_target="tpu_custom_call" | custom-call | tf_op jit(solution)/shard_map/pallas_call | solution.py:352

commit v5 on v4

--- a/solution.py
+++ b/solution.py
@@ -17,7 +17,7 @@
 bf = jnp.bfloat16
 f32 = jnp.float32
 MESH = pl.DeviceIdType.MESH
-UNROLL = 3
+UNROLL = 6
 
 
 def place():
@@ -37,8 +37,8 @@
 ORDER = (1, 2, 3, 0)
 
 
-def kernel(lists_hbm, counts_hbm, span_hbm, row_hbm, k_hbm, v_hbm, q_hbm, do_hbm, dq_ref, ko_ref, vo_ref,
-           lists, counts, span, row, tab_v, tab, kin, vin, q_ref, do_ref, tx, ka, va, part, qT, doT, qr, dor, e_buf, p_buf, pair_buf, dqT, racc, rinv, delta,
+def kernel(lists_hbm, counts_hbm, span_hbm, row_hbm, k_hbm, v_hbm, q_hbm, do_hbm, dq_hbm, ko_ref, vo_ref,
+           lists, counts, span, row, tab_v, tab, kin, vin, dq_ref, q_ref, do_ref, tx, ka, va, part, qT, doT, qr, dor, e_buf, p_buf, pair_buf, dqT, racc, rinv, delta,
            rx0, acc, rxb, rxz, zown, res, rxh,
            s_in, hs, hr, gz_s, gz_r, gy_s, gy_r, gf_s, gf_r, gc_s, gc_r,
            s0, r0, sb, rb, sz, rz, sh, rh):
@@ -72,9 +72,9 @@
     pl.semaphore_wait(barrier, len(near) + NK - 1)
     rows = pl.ds(pl.multiple_of((j % 4) * 32, 32), 32)
     heads = []
-    for d in range(1, NK):
-        h = (j + d) % NK
-        for t in range(2):
+    for t in range(2):
+        for d in range(1, NK):
+            h = (j + d) % NK
             heads.append(send(tx.at[h, t], kva[t].at[2 * i + j // 4, rows, :], hs.at[t, d - 1], hr.at[t, d - 1], (i, h)))
     for t in range(2):
         kva[t][2 * i + j // 4, rows, :] = tx[j, t]
@@ -280,7 +280,7 @@
     loads[2].wait()
     loads[3].wait()
     prepare(0)
-    for cp in heads:
+    for cp in heads[:NK - 1]:
         cp.wait_recv()
     kf, vf = gather(0), gather(1)
     advance(kf)
@@ -305,6 +305,8 @@
     to_scalar.start()
     to_scalar.wait()
     advance(kf)
+    for cp in heads[NK - 1:]:
+        cp.wait_recv()
     advance(vf)
     advance(kf, 2)
     advance(vf)
@@ -331,6 +333,8 @@
     advance(kr)
     advance(vr)
     queries(1, 0, NP)
+    leave = pltpu.make_async_copy(dq_ref, dq_hbm, s_in.at[9])
+    leave.start()
     advance(vr)
     advance(kr, 2)
     advance(vr)
@@ -338,6 +342,7 @@
         pass
     for _ in vr:
         pass
+    leave.wait()
     for cp in sends:
         cp.wait_send()
 
@@ -362,18 +367,18 @@
         kernel,
         out_shape=(jax.ShapeDtypeStruct((2 * B, R), bf), tok, tok),
         in_specs=[hb] * 8,
-        out_specs=[vm] * 3,
+        out_specs=[hb, vm, vm],
         scratch_shapes=[
             V((NB, NBLK), jnp.int32), pltpu.SMEM((NBLK,), jnp.int32), pltpu.SMEM((NBLK,), jnp.int32), V((1, NBLK), jnp.int32),
             V((NB + 8, H), jnp.int32), pltpu.SMEM((NB + 8, H), jnp.int32),
-            V((32, NK * H), bf), V((32, NK * H), bf), V((2 * B, R), bf), V((2 * B, R), bf),
+            V((32, NK * H), bf), V((32, NK * H), bf), V((2 * B, R), bf), V((2 * B, R), bf), V((2 * B, R), bf),
             V((NK, 2, 32, H), bf), V((NBLK, B, H), bf), V((NBLK, B, H), bf), V((2, 2, 4, 4, 2, B, H), bf),
             V((2, H, R), bf), V((2, H, R), bf), V((2, R, H), bf), V((2, R, H), bf),
             V((2, NP, 2 * B, R), f32), V((NP, 2 * B, R), f32), V((2 * NB + 1, B, H), f32), V((H, R), f32),
             V((2, 8, R), f32), V((2, 8, R), f32), V((2, 8, R), f32),
             V((2, 4, 4, 2, B, H), bf), V((2, 4, 4, 2, B, H), bf), V((2, 3, 4, 2, B, H), bf),
             V((2, 3, 2, B, H), bf), V((2, 2, B, H), f32), V((2, NK, 32, H), bf), V((2, NK, 32, H), bf),
-            D((9,)), D((2, 7)), D((2, 7)), D((2, 3)), D((2, 3)), D((2, 2, 4)), D((2, 2, 4)), D((2, 2, 4)), D((2, 2, 4)), D((2, 16)), D((2, 16)),
+            D((10,)), D((2, 7)), D((2, 7)), D((2, 3)), D((2, 3)), D((2, 2, 4)), D((2, 2, 4)), D((2, 2, 4)), D((2, 2, 4)), D((2, 16)), D((2, 16)),
             D((2, 4)), D((2, 4)), D((2, 3, 4)), D((2, 3, 4)), D((2, 3)), D((2, 3)), D((2, 7)), D((2, 7)),
         ],
         compiler_params=pltpu.CompilerParams(collective_id=0, has_side_effects=True, vmem_limit_bytes=62 << 20),

time: 87.6 us -> 85.3 us (0.974)
  Pallas kernels: 86.1 us -> 84.2 us
    pallas_call x1, Pallas kernels: 84.2 us -> 82.3 us  [fused(): pl.pallas_call(kernel, out_shape=(jax.ShapeDtypeStruct((2 * B, R), bf), t...]
where the time goes in v5:
time: 85.3 us; the launch traced here: 84.8 us
  Pallas kernels  84.2 us (99%)
    pallas_call x1, Pallas kernels, fused(): pl.pallas_call(kernel, out_shape=(jax.ShapeDtypeStruct((2 * B, R), bf), t...  82.3 us
    pallas_call x1, Pallas kernels, finish(): pl.pallas_call(finish_kernel, out_shape=tuple((jax.ShapeDtypeStruct(o.sha...  1.93 us

profile of v5, /device:TPU:2, one launch (start us, length us, event | category | flops | bytes accessed | tf_op | source)
XLA Modules:
  0.0 84.8 jit_solution(3575513635393873425)
XLA Ops:
  0.6 82.3 %shard_map.94 = (bf16[256,1024]{1,0:T(8,128)(2,1)}, bf16[32,1024]{1,0:T(8,128)(2,1)}, bf16[32,1024]{1,0:T(8,128)(2,1)}) custom-call(s32[24,64]{1,0:T(8,128)} %bitcast.2, s32[64]{0:T(128)} %counts_hbm.1, s32[64]{0:T(128)} %span_hbm.1, s32[1,64]{1,0:T(1,128)} %bitcast.3, bf16[32,1024]{1,0:T(8,128)(2,1)} %k_hbm.1, bf16[32,1024]{1,0:T(8,128)(2,1)} %v_hbm.1, ...), custom_call_target="tpu_custom_call" | custom-call | tf_op jit(solution)/shard_map/pallas_call | solution.py:366
  82.9 1.9 %shard_map.95 = (bf16[256,1024]{1,0:T(8,128)(2,1)}, bf16[32,1024]{1,0:T(8,128)(2,1)}, bf16[32,1024]{1,0:T(8,128)(2,1)}) custom-call(bf16[256,1024]{1,0:T(8,128)(2,1)} %get-tuple-element.6.a, bf16[32,1024]{1,0:T(8,128)(2,1)} %get-tuple-element.7.b, bf16[32,1024]{1,0:T(8,128)(2,1)} %get-tuple-element.8.c), custom_call_target="tpu_custom_call" | custom-call | tf_op jit(solution)/shard_map/pallas_call | solution.py:357

commit v6 on v5

--- a/solution.py
+++ b/solution.py
@@ -328,8 +328,8 @@
     grads(1, 0, NP)
     kr = reduce(0, ko_ref)
     advance(kr)
-    advance(vr)
     queries(0, 0, NP)
+    advance(vr)
     advance(kr)
     advance(vr)
     queries(1, 0, NP)

time: 85.3 us -> 85.3 us (level)
  no operation moved by 1% of the time
where the time goes in v6:
time: 85.3 us; the launch traced here: 84.8 us
  Pallas kernels  84.2 us (99%)
    pallas_call x1, Pallas kernels, fused(): pl.pallas_call(kernel, out_shape=(jax.ShapeDtypeStruct((2 * B, R), bf), t...  82.3 us
    pallas_call x1, Pallas kernels, finish(): pl.pallas_call(finish_kernel, out_shape=tuple((jax.ShapeDtypeStruct(o.sha...  1.93 us

profile of v6, /device:TPU:2, one launch (start us, length us, event | category | flops | bytes accessed | tf_op | source)
XLA Modules:
  0.0 84.8 jit_solution(11859709638491546417)
XLA Ops:
  0.6 82.3 %shard_map.94 = (bf16[256,1024]{1,0:T(8,128)(2,1)}, bf16[32,1024]{1,0:T(8,128)(2,1)}, bf16[32,1024]{1,0:T(8,128)(2,1)}) custom-call(s32[24,64]{1,0:T(8,128)} %bitcast.2, s32[64]{0:T(128)} %counts_hbm.1, s32[64]{0:T(128)} %span_hbm.1, s32[1,64]{1,0:T(1,128)} %bitcast.3, bf16[32,1024]{1,0:T(8,128)(2,1)} %k_hbm.1, bf16[32,1024]{1,0:T(8,128)(2,1)} %v_hbm.1, ...), custom_call_target="tpu_custom_call" | custom-call | tf_op jit(solution)/shard_map/pallas_call | solution.py:366
  82.9 1.9 %shard_map.95 = (bf16[256,1024]{1,0:T(8,128)(2,1)}, bf16[32,1024]{1,0:T(8,128)(2,1)}, bf16[32,1024]{1,0:T(8,128)(2,1)}) custom-call(bf16[256,1024]{1,0:T(8,128)(2,1)} %get-tuple-element.6.a, bf16[32,1024]{1,0:T(8,128)(2,1)} %get-tuple-element.7.b, bf16[32,1024]{1,0:T(8,128)(2,1)} %get-tuple-element.8.c), custom_call_target="tpu_custom_call" | custom-call | tf_op jit(solution)/shard_map/pallas_call | solution.py:357
